TPU v7x, 32 devices: a whole 2x2x4 slice. The times are simulated.
32 devices in a mesh: row: 8 (over z, core), aux: 4 (over y, x).
Axes of the slice: x: 2, y: 2, z: 4, core: 2. Of those that a mesh axis runs over, the one named last changes fastest.
Arguments:
- factor_ia: float32 [64, 12288], P('row', 'aux'), may hold values from -0.8 to 0.8
- factor_jb: float32 [5120, 12288], P('row', 'aux'), may hold values from -0.8 to 0.8
- denominators: float32 [64, 5120], P(None, 'row'), may hold values from 0.5 to 8
Outputs:
- grad_jb: float32 [5120, 12288], P('row', 'aux')
- grad_ia: float32 [64, 12288], P('row', 'aux')
All inputs are finite; a program needn't handle non-finite values.
Results may differ from a plain program's by a relative error of at most 0.00011.
Values sent between devices are 32-bit elements; how exact they have to be, the bound alone decides.
No kernel may reach another device: no remote copies, remote signals or barrier semaphores. Data moves between devices by JAX's collectives and lax.ppermute only.
A program may use at most 64 MiB of HBM per device.

v0:
```python
import jax
import jax.numpy as jnp
from jax import lax
from jax.sharding import PartitionSpec as P


def per_device(factor_ia, factor_jb, denominators):
    whole_ia = lax.all_gather(factor_ia, "row", axis=0, tiled=True)
    partial_value = lax.dot_general(
        whole_ia,
        factor_jb,
        (((1,), (1,)), ((), ())),
        precision=lax.Precision.HIGHEST,
        preferred_element_type=jnp.float32,
    )
    share_width = denominators.shape[1] // lax.axis_size("aux")
    share_start = lax.axis_index("aux") * share_width
    integral_part = lax.psum_scatter(partial_value, "aux", scatter_dimension=1, tiled=True)
    denom_part = lax.dynamic_slice_in_dim(denominators, share_start, share_width, 1)
    amplitudes = lax.all_gather(integral_part / denom_part, "aux", axis=1, tiled=True)
    grad_jb = lax.dot_general(
        amplitudes,
        whole_ia,
        (((0,), (0,)), ((), ())),
        precision=lax.Precision.HIGHEST,
        preferred_element_type=jnp.float32,
    )
    grad_ia = lax.psum_scatter(
        jnp.dot(
            amplitudes,
            factor_jb,
            precision=lax.Precision.HIGHEST,
            preferred_element_type=jnp.float32,
        ),
        "row",
        scatter_dimension=0,
        tiled=True,
    )
    return (grad_jb, grad_ia)


def solution(mesh):
    return jax.shard_map(
        per_device,
        mesh=mesh,
        in_specs=(P("row", "aux"), P("row", "aux"), P(None, "row")),
        out_specs=(P("row", "aux"), P("row", "aux")),
        check_vma=False,
    )
```

profile of v0, /device:TPU:0, one launch (start us, length us, event | category | flops | bytes accessed | tf_op | source)
XLA Modules:
  0.0 119.1 jit_solution(13380019254326274909)
XLA Ops:
  7.2 0.0 reduce-scatter.7.cloned.1.call-start
  7.2 17.4 %all_gather.6 = f32[64,3072]{1,0:T(8,128)S(1)} all-gather(f32[8,3072]{1,0:T(8,128)} %param.3), channel_id=1, replica_groups=mesh['row'=8,'aux'=4] {'row'}, dimensions={0}, use_global_device_ids=true | all-gather | bytes 884736 | tf_op jit(solution)/shard_map/all_gather | solution.py:8
  24.6 9.2 %convolution_bitcast_fusion = f32[640,64]{1,0:T(8,128)} fusion(f32[64,3072]{1,0:T(8,128)S(1)} %all_gather.6, f32[640,3072]{1,0:T(8,128)} %param.4), kind=kOutput, calls=%fused_computation | convolution fusion | flops 1509949440 | bytes 8814592
  33.8 0.0 reduce-scatter.7.cloned.1.call-update
  33.8 0.0 reduce-scatter.5.cloned.1.call-start
  33.9 25.8 %reduce-scatter.7.cloned.1.call-done = f32[160,64]{1,0:T(8,128)} async-done(((f32[640,64]{1,0:T(8,128)}), f32[160,64]{1,0:T(8,128)}) %reduce-scatter.7.cloned.1.call-update) | async-done | bytes 40976
  59.7 1.0 copy.8
  60.6 1.0 divide_bitcast_fusion
  61.6 9.3 %all-gather = f32[4,160,64]{1,2,0:T(8,128)S(1)} all-gather(f32[1,160,64]{1,2,0:T(8,128)S(1)} %divide_bitcast_fusion), channel_id=1, replica_groups=mesh['row'=8,'aux'=4] {'aux'}, dimensions={0}, use_global_device_ids=true | all-gather | bytes 204800 | tf_op jit(solution)/shard_map/all_gather | solution.py:20
  70.9 0.2 copy.6
  71.1 0.2 reshape.5
  71.3 8.9 %fusion.1 = f32[64,3072]{1,0:T(8,128)} fusion(f32[640,64]{0,1:T(8,128)S(1)} %reshape.5, f32[640,3072]{1,0:T(8,128)} %param.4), kind=kOutput, calls=%fused_computation.3 | convolution fusion | flops 1509949440 | bytes 8814592 | tf_op jit(solution)/shard_map/dot_general | solution.py:29
  80.2 0.0 reduce-scatter.5.cloned.1.call-update
  80.2 8.5 %fusion = f32[640,3072]{1,0:T(8,128)} fusion(f32[640,64]{0,1:T(8,128)S(1)} %reshape.5, f32[64,3072]{1,0:T(8,128)S(1)} %all_gather.6), kind=kOutput, calls=%fused_computation.2 | convolution fusion | flops 1509949440 | bytes 8814592 | tf_op jit(solution)/shard_map/dot_general | solution.py:21
  88.7 23.5 %reduce-scatter.5.cloned.1.call-done = f32[8,3072]{1,0:T(8,128)} async-done(((f32[64,3072]{1,0:T(8,128)}), f32[8,3072]{1,0:T(8,128)}) %reduce-scatter.5.cloned.1.call-update) | async-done | bytes 98320 | tf_op jit(solution)/shard_map/reduce_scatter | solution.py:28
Async XLA Ops:
  7.2 52.5 %reduce-scatter.7.cloned.1.call-start = ((), (), s32[]{:S(2)}) async-start(), calls=%async_computation.3 | async-start | bytes 409600
  33.8 78.4 %reduce-scatter.5.cloned.1.call-start = ((), (), s32[]{:S(2)}) async-start(), calls=%async_computation.2 | async-start | bytes 884736 | tf_op jit(solution)/shard_map/reduce_scatter | solution.py:28
Sparse Core Ops, SparseCore 0:
  34.0 25.6 reduce-scatter.6
  80.4 31.8 reduce-scatter.4
where the time goes:
time: 119 us
  waiting for transfers between devices  49.3 us (41%)
  blocking collectives  26.7 us (22%)
  matrix products  26.6 us (22%)
  between operations  14.1 us (12%)
  local copies, waits for them, and re-layouts  1.31 us (1%)
    unnamed x3, waiting for transfers between devices  25.8 us
    reduce_scatter x1, waiting for transfers between devices, per_device(): lax.psum_scatter(jnp.dot(amplitudes, factor_jb, precision=lax.Precision.H...  23.5 us
    all_gather x1, blocking collectives, per_device(): whole_ia = lax.all_gather(factor_ia, 'row', axis=0, tiled=True)  17.4 us
    all_gather x1, blocking collectives, per_device(): lax.all_gather(integral_part / denom_part, 'aux', axis=1, tiled=True)  9.29 us
    unnamed x1, matrix products  9.18 us
    dot_general x1, matrix products, per_device(): jnp.dot(amplitudes, factor_jb, precision=lax.Precision.HIGHEST, preferred...  8.92 us
    dot_general x1, matrix products, per_device(): lax.dot_general(amplitudes, whole_ia, (((0,), (0,)), ((), ())), precision...  8.48 us
  transfers between devices with their start and end apart: 2, of which 2 were waited for; matrix products, arithmetic and copies ran while one was open for 7% of the time, Pallas kernels for 0%

commit v1 on v0

v1 whole, which is shorter than its diff:
```python
import jax
import jax.numpy as jnp
from jax import lax
from jax.sharding import PartitionSpec as P

HIGH = lax.Precision.HIGH


def swap(x, axis, distance):
    size = lax.axis_size(axis)
    return lax.ppermute(x, axis, [(i, i ^ distance) for i in range(size)])


def dot(a, b, dims):
    return lax.dot_general(a, b, (dims, ((), ())), precision=HIGH, preferred_element_type=jnp.float32)


def per_device(factor_ia, factor_jb, denominators):
    rows = lax.axis_size("row")
    aux = lax.axis_size("aux")
    me = lax.axis_index("row")
    height = factor_ia.shape[0]

    far = [swap(factor_ia, "row", d) for d in range(rows - 2, 0, -2)][::-1]
    even = jnp.stack([factor_ia] + far)
    odd = swap(even, "row", 1)
    whole_ia = jnp.stack([even, odd], axis=1).reshape(rows * height, -1)
    denom = jnp.concatenate(
        [lax.dynamic_slice_in_dim(denominators, (me ^ d) * height, height, 0) for d in range(rows)]
    )

    integrals = dot(whole_ia, factor_jb, ((1,), (1,)))
    step = 1
    while step < aux:
        integrals = integrals + swap(integrals, "aux", step)
        step *= 2
    amplitudes = integrals / denom

    partial = dot(amplitudes, factor_jb, ((1,), (0,))).reshape(rows // 2, 2, height, -1)
    summed = partial[:, 0] + swap(partial[:, 1], "row", 1)
    grad_ia = summed[0]
    for part in [swap(summed[d // 2], "row", d) for d in range(rows - 2, 0, -2)]:
        grad_ia = grad_ia + part
    grad_jb = dot(amplitudes, whole_ia, ((0,), (0,)))
    return (grad_jb, grad_ia)


def solution(mesh):
    return jax.shard_map(
        per_device,
        mesh=mesh,
        in_specs=(P("row", "aux"), P("row", "aux"), P(None, "row")),
        out_specs=(P("row", "aux"), P("row", "aux")),
        check_vma=False,
    )
```

time: 119 us -> 58.6 us (0.49)
  waiting for transfers between devices: 49.3 us -> 21.1 us
  blocking collectives: 26.7 us -> 0 us
  between operations: 14.1 us -> 0.71 us
  starting transfers between devices: 0.08 us -> 13.4 us
  matrix products: 26.6 us -> 18.2 us
  local copies, waits for them, and re-layouts: 1.31 us -> 2.99 us
    all_gather x2 -> x0, blocking collectives: 26.7 us -> none  [the longest x1 17.4 us: per_device(): whole_ia = lax.all_gather(factor_ia, 'row', axis=0, tiled=True)]
    unnamed x3 -> x0, waiting for transfers between devices: 25.8 us -> none
    reduce_scatter x1 -> x0, waiting for transfers between devices: 23.5 us -> none  [per_device(): lax.psum_scatter(jnp.dot(amplitudes, factor_jb, precision=lax.Precision.H...]
    ppermute x0 -> x10, waiting for transfers between devices: none -> 21.1 us  [swap(): return lax.ppermute(x, axis, [(i, i ^ distance) for i in range(size)])]
    ppermute x0 -> x10, starting transfers between devices: none -> 13.4 us  [swap(): return lax.ppermute(x, axis, [(i, i ^ distance) for i in range(size)])]
    unnamed x1 -> x0, matrix products: 9.18 us -> none
    unnamed x2 -> x9, local copies, waits for them, and re-layouts: 1.14 us -> 2.94 us
    dot_general x2 -> x3, matrix products: 17.4 us -> 18.2 us  [dot(): lax.dot_general(a, b, (dims, ((), ())), precision=HIGH, preferred_element...]
  transfers between devices with their start and end apart: 2 -> 10, of which waited for: 2 -> 7; matrix products, arithmetic and copies ran while one was open for 7% -> 14% of each run, Pallas kernels for 0% -> 0%
where the time goes in v1:
time: 58.6 us; the launch traced here: 58.2 us
  waiting for transfers between devices  21.1 us (36%)
  matrix products  18.2 us (31%)
  starting transfers between devices  13.4 us (23%)
  local copies, waits for them, and re-layouts  2.99 us (5%)
  other arithmetic  1.73 us (3%)
  between operations  0.71 us (1%)
    ppermute x10, waiting for transfers between devices, swap(): return lax.ppermute(x, axis, [(i, i ^ distance) for i in range(size)])  21.1 us
    dot_general x3, matrix products, dot(): lax.dot_general(a, b, (dims, ((), ())), precision=HIGH, preferred_element...  18.2 us
    ppermute x10, starting transfers between devices, swap(): return lax.ppermute(x, axis, [(i, i ^ distance) for i in range(size)])  13.4 us
    unnamed x9, local copies, waits for them, and re-layouts  2.94 us
  transfers between devices with their start and end apart: 10, of which 7 were waited for; matrix products, arithmetic and copies ran while one was open for 14% of the time, Pallas kernels for 0%

profile of v1, /device:TPU:0, one launch (start us, length us, event | category | flops | bytes accessed | tf_op | source)
XLA Modules:
  0.0 58.2 jit_solution(10821410572113670264)
XLA Ops:
  0.6 0.0 copy-start
  0.6 3.1 %collective-permute-start = (f32[8,3072]{1,0:T(8,128)}, f32[8,3072]{1,0:T(8,128)S(1)}, u32[]{:S(2)}, u32[]{:S(2)}) collective-permute-start(f32[8,3072]{1,0:T(8,128)} %param.3), channel_id=1, source_target_pairs={{0,8},{4,12},{8,0},{12,4},{16,24},{20,28},{24,16},{28,20},{1,9},{5... | collective-permute-start | bytes 294920 | tf_op jit(solution)/shard_map/ppermute | solution.py:11
  3.8 2.5 %collective-permute-start.2 = (f32[8,3072]{1,0:T(8,128)}, f32[8,3072]{1,0:T(8,128)S(1)}, u32[]{:S(2)}, u32[]{:S(2)}) collective-permute-start(f32[8,3072]{1,0:T(8,128)} %param.3), channel_id=1, source_target_pairs={{0,24},{4,28},{8,16},{12,20},{16,8},{20,12},{24,0},{28,4},{1,25},{... | collective-permute-start | bytes 294920 | tf_op jit(solution)/shard_map/ppermute | solution.py:11
  6.2 0.1 collective-permute-start.1
  6.4 0.4 collective-permute-done
  6.8 5.4 %collective-permute-done.2 = f32[8,3072]{1,0:T(8,128)S(1)} collective-permute-done((f32[8,3072]{1,0:T(8,128)}, f32[8,3072]{1,0:T(8,128)S(1)}, u32[]{:S(2)}, u32[]{:S(2)}) %collective-permute-start.2) | collective-permute-done | bytes 98336 | tf_op jit(solution)/shard_map/ppermute | solution.py:11
  12.1 3.3 %collective-permute-done.1 = f32[8,3072]{1,0:T(8,128)S(1)} collective-permute-done((f32[8,3072]{1,0:T(8,128)}, f32[8,3072]{1,0:T(8,128)S(1)}, u32[]{:S(2)}, u32[]{:S(2)}) %collective-permute-start.1) | collective-permute-done | bytes 98336 | tf_op jit(solution)/shard_map/ppermute | solution.py:11
  15.4 0.9 %fusion.6 = (f32[4,1,8,3072]{3,2,1,0:T(8,128)S(1)}, f32[4,8,3072]{2,1,0:T(8,128)S(1)}) fusion(f32[1,8,3072]{2,1,0:T(8,128)S(1)} %bitcast.46, f32[1,8,3072]{2,1,0:T(8,128)S(1)} %bitcast.47, f32[1,8,3072]{2,1,0:T(8,128)S(1)} %bitcast.45, f32[1,8,3072]{2,1,0:T(8,128)} %bitcast.44), kind=kLoop, calls=%fused_computation.23 | loop fusion | flops 294912 | bytes 1179648 | tf_op jit(solution)/shard_map/stack | solution.py:27
  16.4 0.1 collective-permute-start.3
  16.4 0.7 %dynamic-slice_dynamic-update-slice_fusion.7 = f32[64,640]{1,0:T(8,128)S(1)} fusion(f32[64,640]{1,0:T(8,128)} %param.5, s32[]{:T(128)S(6)} %select_n.24), kind=kLoop, calls=%fused_computation.20 | loop fusion | bytes 40964
  17.2 0.7 %dynamic-slice_dynamic-update-slice_fusion.6 = f32[64,640]{1,0:T(8,128)S(1)} fusion(f32[64,640]{1,0:T(8,128)S(1)} %dynamic-slice_dynamic-update-slice_fusion.7, f32[64,640]{1,0:T(8,128)} %param.5, s32[]{:T(128)S(6)} %select_n.25), kind=kLoop, calls=%fused_computation.19 | loop fusion | bytes 40964
  17.9 0.7 %dynamic-slice_dynamic-update-slice_fusion.5 = f32[64,640]{1,0:T(8,128)S(1)} fusion(f32[64,640]{1,0:T(8,128)S(1)} %dynamic-slice_dynamic-update-slice_fusion.6, f32[64,640]{1,0:T(8,128)} %param.5, s32[]{:T(128)S(6)} %select_n.26), kind=kLoop, calls=%fused_computation.18 | loop fusion | bytes 40964
  18.6 0.7 %dynamic-slice_dynamic-update-slice_fusion.4 = f32[64,640]{1,0:T(8,128)S(1)} fusion(f32[64,640]{1,0:T(8,128)S(1)} %dynamic-slice_dynamic-update-slice_fusion.5, f32[64,640]{1,0:T(8,128)} %param.5, s32[]{:T(128)S(6)} %select_n.27), kind=kLoop, calls=%fused_computation.17 | loop fusion | bytes 40964
  19.4 0.0 collective-permute-done.3
  19.4 0.1 pad_maximum_fusion
  19.4 6.9 %fusion.7 = f32[64,640]{1,0:T(8,128)S(1)} fusion(f32[64,3072]{1,0:T(8,128)S(1)} %bitcast.39, f32[640,3072]{1,0:T(8,128)} %param.4), kind=kOutput, calls=%fused_computation.24 | convolution fusion | flops 754974720 | bytes 8814592 | tf_op jit(solution)/shard_map/dot_general | solution.py:15
  26.4 1.6 %collective-permute-start.4 = (f32[64,640]{1,0:T(8,128)S(1)}, f32[64,640]{1,0:T(8,128)S(1)}, u32[]{:S(2)}, u32[]{:S(2)}) collective-permute-start(f32[64,640]{1,0:T(8,128)S(1)} %fusion.7), channel_id=1, source_target_pairs={{0,1},{1,0},{2,3},{3,2},{4,5},{5,4},{6,7},{7,6},{8,9},{9,8},{10,11... | collective-permute-start | bytes 491528 | tf_op jit(solution)/shard_map/ppermute | solution.py:11
  27.9 0.0 copy-done
  27.9 5.1 %collective-permute-done.4 = f32[64,640]{1,0:T(8,128)S(1)} collective-permute-done((f32[64,640]{1,0:T(8,128)S(1)}, f32[64,640]{1,0:T(8,128)S(1)}, u32[]{:S(2)}, u32[]{:S(2)}) %collective-permute-start.4) | collective-permute-done | bytes 163872 | tf_op jit(solution)/shard_map/ppermute | solution.py:11
  33.0 1.6 %collective-permute-start.5 = (f32[64,640]{1,0:T(8,128)S(1)}, f32[64,640]{1,0:T(8,128)S(1)}, u32[]{:S(2)}, u32[]{:S(2)}) collective-permute-start(f32[64,640]{1,0:T(8,128)S(1)} %add.42), channel_id=1, source_target_pairs={{0,2},{1,3},{2,0},{3,1},{4,6},{5,7},{6,4},{7,5},{8,10},{9,11},{10,... | collective-permute-start | bytes 491528 | tf_op jit(solution)/shard_map/ppermute | solution.py:11
  34.6 4.2 %collective-permute-done.5 = f32[64,640]{1,0:T(8,128)S(1)} collective-permute-done((f32[64,640]{1,0:T(8,128)S(1)}, f32[64,640]{1,0:T(8,128)S(1)}, u32[]{:S(2)}, u32[]{:S(2)}) %collective-permute-start.5) | collective-permute-done | bytes 163872 | tf_op jit(solution)/shard_map/ppermute | solution.py:11
  38.9 5.8 %fusion.4 = f32[64,3072]{1,0:T(8,128)S(1)} fusion(f32[640,3072]{1,0:T(8,128)} %param.4, f32[64,640]{1,0:T(8,128)S(1)} %dynamic-slice_dynamic-update-slice_fusion, f32[64,640]{1,0:T(8,128)S(1)} %add.42, f32[64,640]{1,0:T(8,128)S(1)} %collective-permute-done.5), kind=kOutput, calls=%fused_computation.21 | convolution fusion | flops 755056640 | bytes 9142272 | tf_op jit(solution)/shard_map/dot_general | solution.py:15
  44.7 0.1 collective-permute-start.6
  44.8 1.7 %collective-permute-done.6 = f32[4,8,3072]{2,1,0:T(8,128)S(1)} collective-permute-done((f32[4,8,3072]{2,1,0:T(8,128)S(1)}, f32[4,8,3072]{2,1,0:T(8,128)S(1)}, u32[]{:S(2)}, u32[]{:S(2)}) %collective-permute-start.6) | collective-permute-done | bytes 393248 | tf_op jit(solution)/shard_map/ppermute | solution.py:11
  46.5 0.1 fusion
  46.6 2.7 %collective-permute-start.7 = (f32[8,3072]{1,0:T(8,128)S(1)}, f32[8,3072]{1,0:T(8,128)S(1)}, u32[]{:S(2)}, u32[]{:S(2)}) collective-permute-start(f32[8,3072]{1,0:T(8,128)S(1)} %get-tuple-element.2), channel_id=1, source_target_pairs={{0,24},{4,28},{8,16},{12,20},{16,8},{20,12},{24,0},{28,4},{1,25},{... | collective-permute-start | bytes 294920 | tf_op jit(solution)/shard_map/ppermute | solution.py:11
  49.3 0.0 collective-permute-start.9
  49.3 1.8 %collective-permute-start.8 = (f32[8,3072]{1,0:T(8,128)S(1)}, f32[8,3072]{1,0:T(8,128)S(1)}, u32[]{:S(2)}, u32[]{:S(2)}) collective-permute-start(f32[8,3072]{1,0:T(8,128)S(1)} %get-tuple-element.4), channel_id=1, source_target_pairs={{0,16},{4,20},{8,24},{12,28},{16,0},{20,4},{24,8},{28,12},{1,17},{... | collective-permute-start | bytes 294920 | tf_op jit(solution)/shard_map/ppermute | solution.py:11
  51.1 5.4 %fusion.5 = f32[640,3072]{1,0:T(8,128)} fusion(f32[64,3072]{1,0:T(8,128)S(1)} %bitcast.40, f32[64,640]{1,0:T(8,128)S(1)} %dynamic-slice_dynamic-update-slice_fusion, f32[64,640]{1,0:T(8,128)S(1)} %add.42, f32[64,640]{1,0:T(8,128)S(1)} %collective-permute-done.5), kind=kOutput, calls=%fused_computation.22 | convolution fusion | flops 755056640 | bytes 9142272 | tf_op jit(solution)/shard_map/dot_general | solution.py:15
  56.5 0.0 collective-permute-done.7
  56.5 1.0 %collective-permute-done.9 = f32[8,3072]{1,0:T(8,128)S(1)} collective-permute-done((f32[8,3072]{1,0:T(8,128)S(1)}, f32[8,3072]{1,0:T(8,128)S(1)}, u32[]{:S(2)}, u32[]{:S(2)}) %collective-permute-start.9) | collective-permute-done | bytes 98336 | tf_op jit(solution)/shard_map/ppermute | solution.py:11
  57.5 0.0 collective-permute-done.8
  57.5 0.7 %fusion.3 = f32[8,3072]{1,0:T(8,128)} fusion(f32[8,3072]{1,0:T(8,128)S(1)} %collective-permute-done.9, f32[8,3072]{1,0:T(8,128)S(1)} %collective-permute-done.8, f32[8,3072]{1,0:T(8,128)S(1)} %collective-permute-done.7, f32[4,8,3072]{2,1,0:T(8,128)S(1)} %fusion), kind=kLoop, calls=%fused_computation.12 | loop fusion | flops 73728 | bytes 491520 | tf_op jit(solution)/shard_map/add | solution.py:43
  (7 shorter events, 0.1 us)
Async XLA Ops:
  0.6 27.3 %copy-start = (f32[64,640]{1,0:T(8,128)S(1)}, f32[64,640]{1,0:T(8,128)}, u32[]{:S(2)}) copy-start(f32[64,640]{1,0:T(8,128)} %param.5) | copy-start | bytes 491524
  0.6 6.1 %collective-permute-start = (f32[8,3072]{1,0:T(8,128)}, f32[8,3072]{1,0:T(8,128)S(1)}, u32[]{:S(2)}, u32[]{:S(2)}) collective-permute-start(f32[8,3072]{1,0:T(8,128)} %param.3), channel_id=1, source_target_pairs={{0,8},{4,12},{8,0},{12,4},{16,24},{20,28},{24,16},{28,20},{1,9},{5... | collective-permute-start | bytes 294920 | tf_op jit(solution)/shard_map/ppermute | solution.py:11
  3.8 8.4 %collective-permute-start.2 = (f32[8,3072]{1,0:T(8,128)}, f32[8,3072]{1,0:T(8,128)S(1)}, u32[]{:S(2)}, u32[]{:S(2)}) collective-permute-start(f32[8,3072]{1,0:T(8,128)} %param.3), channel_id=1, source_target_pairs={{0,24},{4,28},{8,16},{12,20},{16,8},{20,12},{24,0},{28,4},{1,25},{... | collective-permute-start | bytes 294920 | tf_op jit(solution)/shard_map/ppermute | solution.py:11
  6.2 9.2 %collective-permute-start.1 = (f32[8,3072]{1,0:T(8,128)}, f32[8,3072]{1,0:T(8,128)S(1)}, u32[]{:S(2)}, u32[]{:S(2)}) collective-permute-start(f32[8,3072]{1,0:T(8,128)} %param.3), channel_id=1, source_target_pairs={{0,16},{4,20},{8,24},{12,28},{16,0},{20,4},{24,8},{28,12},{1,17},{... | collective-permute-start | bytes 294920 | tf_op jit(solution)/shard_map/ppermute | solution.py:11
  16.4 3.0 %collective-permute-start.3 = (f32[4,8,3072]{2,1,0:T(8,128)S(1)}, f32[4,8,3072]{2,1,0:T(8,128)S(1)}, u32[]{:S(2)}, u32[]{:S(2)}) collective-permute-start(f32[4,8,3072]{2,1,0:T(8,128)S(1)} %get-tuple-element.6), channel_id=1, source_target_pairs={{0,4},{4,0},{8,12},{12,8},{16,20},{20,16},{24,28},{28,24},{1,5},{5... | collective-permute-start | bytes 1179656 | tf_op jit(solution)/shard_map/ppermute | solution.py:11
  26.4 6.7 %collective-permute-start.4 = (f32[64,640]{1,0:T(8,128)S(1)}, f32[64,640]{1,0:T(8,128)S(1)}, u32[]{:S(2)}, u32[]{:S(2)}) collective-permute-start(f32[64,640]{1,0:T(8,128)S(1)} %fusion.7), channel_id=1, source_target_pairs={{0,1},{1,0},{2,3},{3,2},{4,5},{5,4},{6,7},{7,6},{8,9},{9,8},{10,11... | collective-permute-start | bytes 491528 | tf_op jit(solution)/shard_map/ppermute | solution.py:11
  33.0 5.8 %collective-permute-start.5 = (f32[64,640]{1,0:T(8,128)S(1)}, f32[64,640]{1,0:T(8,128)S(1)}, u32[]{:S(2)}, u32[]{:S(2)}) collective-permute-start(f32[64,640]{1,0:T(8,128)S(1)} %add.42), channel_id=1, source_target_pairs={{0,2},{1,3},{2,0},{3,1},{4,6},{5,7},{6,4},{7,5},{8,10},{9,11},{10,... | collective-permute-start | bytes 491528 | tf_op jit(solution)/shard_map/ppermute | solution.py:11
  44.7 1.8 %collective-permute-start.6 = (f32[4,8,3072]{2,1,0:T(8,128)S(1)}, f32[4,8,3072]{2,1,0:T(8,128)S(1)}, u32[]{:S(2)}, u32[]{:S(2)}) collective-permute-start(f32[4,8,3072]{2,1,0:T(8,128)S(1)} %slice_bitcast_fusion), channel_id=1, source_target_pairs={{0,4},{4,0},{8,12},{12,8},{16,20},{20,16},{24,28},{28,24},{1,5},{5... | collective-permute-start | bytes 1179656 | tf_op jit(solution)/shard_map/ppermute | solution.py:11
  46.6 9.9 %collective-permute-start.7 = (f32[8,3072]{1,0:T(8,128)S(1)}, f32[8,3072]{1,0:T(8,128)S(1)}, u32[]{:S(2)}, u32[]{:S(2)}) collective-permute-start(f32[8,3072]{1,0:T(8,128)S(1)} %get-tuple-element.2), channel_id=1, source_target_pairs={{0,24},{4,28},{8,16},{12,20},{16,8},{20,12},{24,0},{28,4},{1,25},{... | collective-permute-start | bytes 294920 | tf_op jit(solution)/shard_map/ppermute | solution.py:11
  49.3 8.2 %collective-permute-start.9 = (f32[8,3072]{1,0:T(8,128)S(1)}, f32[8,3072]{1,0:T(8,128)S(1)}, u32[]{:S(2)}, u32[]{:S(2)}) collective-permute-start(f32[8,3072]{1,0:T(8,128)S(1)} %get-tuple-element.3), channel_id=1, source_target_pairs={{0,8},{4,12},{8,0},{12,4},{16,24},{20,28},{24,16},{28,20},{1,9},{5... | collective-permute-start | bytes 294920 | tf_op jit(solution)/shard_map/ppermute | solution.py:11
  49.3 8.2 %collective-permute-start.8 = (f32[8,3072]{1,0:T(8,128)S(1)}, f32[8,3072]{1,0:T(8,128)S(1)}, u32[]{:S(2)}, u32[]{:S(2)}) collective-permute-start(f32[8,3072]{1,0:T(8,128)S(1)} %get-tuple-element.4), channel_id=1, source_target_pairs={{0,16},{4,20},{8,24},{12,28},{16,0},{20,4},{24,8},{28,12},{1,17},{... | collective-permute-start | bytes 294920 | tf_op jit(solution)/shard_map/ppermute | solution.py:11

commit v2 on v1

v2 whole, which is shorter than its diff:
```python
import jax
import jax.numpy as jnp
from jax import lax
from jax.experimental import pallas as pl
from jax.experimental.pallas import tpu as pltpu
from jax.sharding import PartitionSpec as P


F32, BF16 = jnp.float32, jnp.bfloat16
VMEM = pl.BlockSpec(memory_space=pltpu.VMEM)
HBM = pl.BlockSpec(memory_space=pltpu.HBM)
MIB = 1 << 20
TILE = 128
FIRST = 3


def swap(x, axis, distance):
    size = lax.axis_size(axis)
    return lax.ppermute(x, axis, [(i, i ^ distance) for i in range(size)])


def split(x):
    hi = x.astype(BF16)
    return hi, (x - hi.astype(F32)).astype(BF16)


def mxu(a, b, dims):
    return lax.dot_general(a, b, (dims, ((), ())), preferred_element_type=F32)


def width_of(size, most):
    fits = [w for w in range(128, min(size, most) + 1, 128) if size % w == 0]
    return fits[-1] if fits else size


def prepare(factor_jb):
    height, width = factor_jb.shape
    pieces = [p for p in (8, 4, 2, 1) if height % (16 * p) == 0][0]
    piece = height // pieces

    def kernel(jb, hi, lo, held, sems):
        def copy(p):
            at = pl.ds(p * piece, piece)
            return pltpu.make_async_copy(jb.at[at], held.at[at], sems.at[p])

        for p in range(pieces):
            copy(p).start()
        for p in range(pieces):
            copy(p).wait()

            @pl.loop(0, piece, step=16)
            def _(r, p=p):
                at = pl.ds(p * piece + r, 16)
                hi[at], lo[at] = split(held[at])

    out = jax.ShapeDtypeStruct((height, width), BF16)
    return pl.pallas_call(
        kernel,
        name="prepare",
        out_shape=(out, out),
        in_specs=[HBM],
        out_specs=(VMEM, VMEM),
        scratch_shapes=[pltpu.VMEM((height, width), F32), pltpu.SemaphoreType.DMA((pieces,))],
        compiler_params=pltpu.CompilerParams(vmem_limit_bytes=44 * MIB),
        cost_estimate=pl.CostEstimate(flops=4 * height * width, bytes_accessed=4 * height * width, transcendentals=0),
    )(factor_jb)


def integral_share(blocks, jb_hi, jb_lo, columns, parts=None):
    n = len(blocks)
    height, width = blocks[0].shape
    rows = n * height
    start, count = columns

    def kernel(*refs):
        block_refs, (hi, lo, out, parts) = refs[:n], refs[n : n + 4]
        for pair in range(n // 2):
            x = jnp.concatenate([block_refs[2 * pair][...], block_refs[2 * pair + 1][...]])
            a, b = split(x)
            at = 2 * height * pair
            parts[pl.ds(at, 2 * height)] = a
            parts[pl.ds(rows + at, 2 * height)] = b
        multiply(parts, hi, lo, out)

    def again(parts, hi, lo, out):
        multiply(parts, hi, lo, out)

    def multiply(parts, hi, lo, out):
        for t in range(0, count, TILE):
            at = pl.ds(start + t, TILE)
            both = mxu(parts[...], hi[at], ((1,), (1,)))
            rest = mxu(parts[pl.ds(0, rows)], lo[at], ((1,), (1,)))
            out[:, pl.ds(t, TILE)] = both[:rows] + (both[rows:] + rest)

    out = jax.ShapeDtypeStruct((rows, count), F32)
    stacked = jax.ShapeDtypeStruct((2 * rows, width), BF16)
    first = parts is None
    return pl.pallas_call(
        kernel if first else again,
        out_shape=(out, stacked) if first else out,
        in_specs=[VMEM] * (n + 2 if first else 3),
        out_specs=(VMEM, VMEM) if first else VMEM,
        compiler_params=pltpu.CompilerParams(vmem_limit_bytes=30 * MIB),
        cost_estimate=pl.CostEstimate(flops=6 * rows * width * count, bytes_accessed=MIB, transcendentals=0),
    )(*(blocks if first else [parts]), jb_hi, jb_lo)


def gradient_share(mine, theirs, denominators, jb_hi, jb_lo, distances, columns, height, before=None):
    rows = mine.shape[0]
    width = jb_hi.shape[1]
    n = len(distances)
    tile = width_of(width, 512)
    start, count = columns
    last = before is not None

    def kernel(*refs):
        mine, theirs, denom, hi, lo = refs[:5]
        parts, *outs, amp = refs[5 + last :]
        me = lax.axis_index("row")
        for slot, d in enumerate(distances):
            at = pl.multiple_of((me ^ d) * height, height)
            here = pl.ds(slot * height, height)
            amp[here] = (mine[here] + theirs[here]) / denom[pl.ds(at, height), pl.ds(start, count)]
        a, b = split(amp[...])
        parts[pl.ds(0, rows)] = a
        parts[pl.ds(rows, rows)] = b
        for t in range(width // tile):
            at = pl.ds(t * tile, tile)
            both = mxu(parts[...], hi[pl.ds(start, count), at], ((1,), (0,)))
            rest = mxu(parts[pl.ds(0, rows)], lo[pl.ds(start, count), at], ((1,), (0,)))
            total = both[:rows] + (both[rows:] + rest)
            if last:
                total = refs[5][:, at] + total
                for slot in range(n):
                    outs[slot % 2][slot // 2, :, at] = total[slot * height : (slot + 1) * height]
            else:
                outs[0][:, at] = total

    half = jax.ShapeDtypeStruct((n // 2, height, width), F32)
    outs = (half, half) if last else (jax.ShapeDtypeStruct((rows, width), F32),)
    args = (mine, theirs, denominators, jb_hi, jb_lo) + ((before,) if last else ())
    return pl.pallas_call(
        kernel,
        out_shape=(jax.ShapeDtypeStruct((2 * rows, count), BF16), *outs),
        in_specs=[VMEM] * len(args),
        out_specs=(VMEM,) * (1 + len(outs)),
        scratch_shapes=[pltpu.VMEM((rows, count), F32)],
        compiler_params=pltpu.CompilerParams(vmem_limit_bytes=30 * MIB),
        cost_estimate=pl.CostEstimate(flops=6 * rows * width * count, bytes_accessed=MIB, transcendentals=0),
    )(*args)


def gradient_jb(amp_parts, ia_parts):
    rows, width = ia_parts.shape[0] // 2, ia_parts.shape[1]
    first, second = (a.shape[1] // TILE for a in amp_parts)

    def kernel(one, two, ia, out):
        amp = jnp.where(pl.program_id(0) < first, one[...].astype(F32), two[...].astype(F32))
        a_hi, a_lo = amp[:rows], amp[rows:]
        i_hi, i_lo = ia[pl.ds(0, rows)], ia[pl.ds(rows, rows)]
        left = jnp.concatenate([a_hi, a_lo, a_hi]).T.astype(BF16)
        out[...] = mxu(left, jnp.concatenate([i_hi, i_hi, i_lo]), ((1,), (0,)))

    return pl.pallas_call(
        kernel,
        name="gradient_jb",
        grid=(first + second,),
        out_shape=jax.ShapeDtypeStruct(((first + second) * TILE, width), F32),
        in_specs=[
            pl.BlockSpec((2 * rows, TILE), lambda t: (0, jnp.minimum(t, first - 1))),
            pl.BlockSpec((2 * rows, TILE), lambda t: (0, jnp.maximum(t - first, 0))),
            pl.BlockSpec((2 * rows, width), lambda t: (0, 0)),
        ],
        out_specs=pl.BlockSpec((TILE, width), lambda t: (t, 0)),
        compiler_params=pltpu.CompilerParams(vmem_limit_bytes=30 * MIB),
        cost_estimate=pl.CostEstimate(
            flops=6 * rows * width * (first + second) * TILE,
            bytes_accessed=4 * width * (first + second) * TILE,
            transcendentals=0,
        ),
    )(*amp_parts, ia_parts)


def chip_order(rows):
    chips = rows // 2
    return [k for k in (2, 1, *range(3, chips)) if k < chips]


def aux_order(aux, chunk):
    steps = [1 << b for b in range(aux.bit_length() - 1)]
    return steps[::-1] if chunk else steps


def per_device(factor_ia, factor_jb, denominators):
    rows = lax.axis_size("row")
    aux = lax.axis_size("aux")
    height = factor_ia.shape[0]
    tiles = factor_jb.shape[0] // TILE
    cut = FIRST * tiles // 5 * TILE
    chunks = [(0, cut), (cut, tiles * TILE - cut)]

    blocks = {0: factor_ia}
    for k in chip_order(rows):
        blocks[2 * k] = swap(factor_ia, "row", 2 * k)
    for d in range(0, rows, 2):
        blocks[d + 1] = swap(blocks[d], "row", 1)
    jb_hi, jb_lo = prepare(factor_jb)

    ordered = [blocks[d] for d in range(rows)]
    share0, ia_parts = integral_share(ordered, jb_hi, jb_lo, chunks[0])
    share1 = integral_share(ordered, jb_hi, jb_lo, chunks[1], ia_parts)
    amp_parts, outs = [], [None]
    for c, share in enumerate((share0, share1)):
        *steps, step = aux_order(aux, c)
        for s in steps:
            share = share + swap(share, "aux", s)
        theirs = swap(share, "aux", step)
        amp, *outs = gradient_share(share, theirs, denominators, jb_hi, jb_lo, range(rows), chunks[c], height, outs[0])
        amp_parts.append(amp)

    odd, even = outs[1], outs[0]
    summed = even + swap(odd, "row", 1)
    grad_ia = summed[0]
    for k in chip_order(rows):
        grad_ia = grad_ia + swap(summed[k], "row", 2 * k)
    grad_jb = gradient_jb(amp_parts, ia_parts)
    return (grad_jb, grad_ia)


def solution(mesh):
    return jax.shard_map(
        per_device,
        mesh=mesh,
        in_specs=(P("row", "aux"), P("row", "aux"), P(None, "row")),
        out_specs=(P("row", "aux"), P("row", "aux")),
        check_vma=False,
    )
```

time: 58.6 us -> 51.7 us (0.88)
  matrix products: 18.2 us -> 0 us
  Pallas kernels: 0 us -> 12.5 us
  local copies, waits for them, and re-layouts: 2.99 us -> 0.03 us
  starting transfers between devices: 13.4 us -> 16.1 us
  other arithmetic: 1.73 us -> 0.72 us
    dot_general x3 -> x0, matrix products: 18.2 us -> none  [dot(): lax.dot_general(a, b, (dims, ((), ())), precision=HIGH, preferred_element...]
    pallas_call x0 -> x6, Pallas kernels: none -> 12.5 us  [the longest x1 4.71 us: gradient_jb(): pl.pallas_call(kernel, name='gradient_jb', grid=(first + second,), out_sh...]
    unnamed x9 -> x4, local copies, waits for them, and re-layouts: 2.94 us -> 0.01 us
    ppermute x10 -> x15, starting transfers between devices: 13.4 us -> 16.1 us  [swap(): return lax.ppermute(x, axis, [(i, i ^ distance) for i in range(size)])]
    another operation x2 -> x0, other arithmetic: 1 us -> none  [per_device(): whole_ia = jnp.stack([even, odd], axis=1).reshape(rows * height, -1)]
    ppermute x10 -> x15, waiting for transfers between devices: 21.1 us -> 21.5 us  [swap(): return lax.ppermute(x, axis, [(i, i ^ distance) for i in range(size)])]
  transfers between devices with their start and end apart: 10 -> 15, of which waited for: 7 -> 8; matrix products, arithmetic and copies ran while one was open for 14% -> 0% of each run, Pallas kernels for 0% -> 20%
where the time goes in v2:
time: 51.7 us; the launch traced here: 51.6 us
  waiting for transfers between devices  21.5 us (42%)
  starting transfers between devices  16.1 us (31%)
  Pallas kernels  12.5 us (24%)
  between operations  0.76 us (1%)
  other arithmetic  0.72 us (1%)
    ppermute x15, waiting for transfers between devices, swap(): return lax.ppermute(x, axis, [(i, i ^ distance) for i in range(size)])  21.5 us
    ppermute x15, starting transfers between devices, swap(): return lax.ppermute(x, axis, [(i, i ^ distance) for i in range(size)])  16.1 us
    pallas_call x1, Pallas kernels, gradient_jb(): pl.pallas_call(kernel, name='gradient_jb', grid=(first + second,), out_sh...  4.71 us
    pallas_call x1, Pallas kernels, prepare(): pl.pallas_call(kernel, name='prepare', out_shape=(out, out), in_specs=[HB...  3.48 us
    pallas_call x2, Pallas kernels, integral_share(): pl.pallas_call(kernel if first else again, out_shape=(out, stacked) if fi...  2.6 us
    pallas_call x2, Pallas kernels, gradient_share(): pl.pallas_call(kernel, out_shape=(jax.ShapeDtypeStruct((2 * rows, count),...  1.67 us
  transfers between devices with their start and end apart: 15, of which 8 were waited for; matrix products, arithmetic and copies ran while one was open for 0% of the time, Pallas kernels for 20%

profile of v2, /device:TPU:0, one launch (start us, length us, event | category | flops | bytes accessed | tf_op | source)
XLA Modules:
  0.0 51.6 jit_solution(10239096396401017463)
XLA Ops:
  0.6 0.0 copy-start.1
  0.6 3.1 %collective-permute-start.1 = (f32[8,3072]{1,0:T(8,128)}, f32[8,3072]{1,0:T(8,128)S(1)}, u32[]{:S(2)}, u32[]{:S(2)}) collective-permute-start(f32[8,3072]{1,0:T(8,128)} %refs_0_.1), channel_id=1, source_target_pairs={{0,8},{4,12},{8,0},{12,4},{16,24},{20,28},{24,16},{28,20},{1,9},{5... | collective-permute-start | bytes 294920 | tf_op jit(solution)/shard_map/ppermute | solution.py:19
  3.8 2.6 %collective-permute-start.3 = (f32[8,3072]{1,0:T(8,128)}, f32[8,3072]{1,0:T(8,128)S(1)}, u32[]{:S(2)}, u32[]{:S(2)}) collective-permute-start(f32[8,3072]{1,0:T(8,128)} %refs_0_.1), channel_id=1, source_target_pairs={{0,16},{4,20},{8,24},{12,28},{16,0},{20,4},{24,8},{28,12},{1,17},{... | collective-permute-start | bytes 294920 | tf_op jit(solution)/shard_map/ppermute | solution.py:19
  6.3 0.0 collective-permute-start.5
  6.3 0.0 collective-permute-start
  6.4 0.4 collective-permute-done.1.refs_2_
  6.8 0.1 collective-permute-start.2
  6.9 7.5 %collective-permute-done.3.refs_4_ = f32[8,3072]{1,0:T(8,128)S(1)} collective-permute-done((f32[8,3072]{1,0:T(8,128)}, f32[8,3072]{1,0:T(8,128)S(1)}, u32[]{:S(2)}, u32[]{:S(2)}) %collective-permute-start.3) | collective-permute-done | bytes 98336 | tf_op jit(solution)/shard_map/ppermute | solution.py:19
  14.4 0.0 collective-permute-start.4
  14.4 0.0 collective-permute-done.5.refs_6_
  14.4 0.5 collective-permute-start.6
  14.9 3.5 %prepare.1 = (bf16[640,3072]{1,0:T(8,128)(2,1)S(1)}, bf16[640,3072]{1,0:T(8,128)(2,1)S(1)}) custom-call(f32[640,3072]{1,0:T(8,128)} %jb.1), custom_call_target="tpu_custom_call" | custom-call | flops 7864320 | bytes 7864320 | tf_op jit(solution)/shard_map/prepare/pallas_call | solution.py:57
  18.4 0.0 collective-permute-done.refs_1_
  18.4 0.0 collective-permute-done.2.refs_3_
  18.4 0.0 collective-permute-done.4.refs_5_
  18.4 0.0 collective-permute-done.6.refs_7_
  18.5 0.0 copy-done.1
  18.5 0.0 copy-start
  18.5 1.5 %shard_map.50 = (f32[64,384]{1,0:T(8,128)S(1)}, bf16[128,3072]{1,0:T(8,128)(2,1)S(1)}) custom-call(f32[8,3072]{1,0:T(8,128)S(1)} %copy-done.1, f32[8,3072]{1,0:T(8,128)S(1)} %collective-permute-done.refs_1_, f32[8,3072]{1,0:T(8,128)S(1)} %collective-permute-done.1.refs_2_, f32[8,3072]{1,0:T(8,128)S(1)} %collective-permute-done.2.refs_3_, ...), custom_call_target="tpu_custom_call" | custom-call | flops 452984832 | bytes 1048576 | tf_op jit(solution)/shard_map/pallas_call | solution.py:98
  20.0 1.6 %collective-permute-start.7 = (f32[64,384]{1,0:T(8,128)S(1)}, f32[64,384]{1,0:T(8,128)S(1)}, u32[]{:S(2)}, u32[]{:S(2)}) collective-permute-start(f32[64,384]{1,0:T(8,128)S(1)} %get-tuple-element.13), channel_id=1, source_target_pairs={{0,1},{1,0},{2,3},{3,2},{4,5},{5,4},{6,7},{7,6},{8,9},{9,8},{10,11... | collective-permute-start | bytes 294920 | tf_op jit(solution)/shard_map/ppermute | solution.py:19
  21.6 3.2 %collective-permute-done.7 = f32[64,384]{1,0:T(8,128)S(1)} collective-permute-done((f32[64,384]{1,0:T(8,128)S(1)}, f32[64,384]{1,0:T(8,128)S(1)}, u32[]{:S(2)}, u32[]{:S(2)}) %collective-permute-start.7) | collective-permute-done | bytes 98336 | tf_op jit(solution)/shard_map/ppermute | solution.py:19
  24.8 1.6 %collective-permute-start.8 = (f32[64,384]{1,0:T(8,128)S(1)}, f32[64,384]{1,0:T(8,128)S(1)}, u32[]{:S(2)}, u32[]{:S(2)}) collective-permute-start(f32[64,384]{1,0:T(8,128)S(1)} %add.18.refs_0_), channel_id=1, source_target_pairs={{0,2},{1,3},{2,0},{3,1},{4,6},{5,7},{6,4},{7,5},{8,10},{9,11},{10,... | collective-permute-start | bytes 294920 | tf_op jit(solution)/shard_map/ppermute | solution.py:19
  26.4 1.1 %shard_map.52 = f32[64,256]{1,0:T(8,128)S(1)} custom-call(bf16[128,3072]{1,0:T(8,128)(2,1)S(1)} %get-tuple-element.15.parts.ia, bf16[640,3072]{1,0:T(8,128)(2,1)S(1)} %get-tuple-element.11.refs_8_.refs_3_.hi, bf16[640,3072]{1,0:T(8,128)(2,1)S(1)} %get-tuple-element.12.refs_9_.refs_4_.lo), custom_call_target="tpu_custom_call" | custom-call | flops 301989888 | bytes 1048576 | tf_op jit(solution)/shard_map/pallas_call | solution.py:98
  27.5 0.6 %collective-permute-start.9 = (f32[64,256]{1,0:T(8,128)S(1)}, f32[64,256]{1,0:T(8,128)S(1)}, u32[]{:S(2)}, u32[]{:S(2)}) collective-permute-start(f32[64,256]{1,0:T(8,128)S(1)} %shard_map.52), channel_id=1, source_target_pairs={{0,2},{1,3},{2,0},{3,1},{4,6},{5,7},{6,4},{7,5},{8,10},{9,11},{10,... | collective-permute-start | bytes 196616 | tf_op jit(solution)/shard_map/ppermute | solution.py:19
  28.0 3.8 %collective-permute-done.9 = f32[64,256]{1,0:T(8,128)S(1)} collective-permute-done((f32[64,256]{1,0:T(8,128)S(1)}, f32[64,256]{1,0:T(8,128)S(1)}, u32[]{:S(2)}, u32[]{:S(2)}) %collective-permute-start.9) | collective-permute-done | bytes 65568 | tf_op jit(solution)/shard_map/ppermute | solution.py:19
  31.8 1.6 %collective-permute-start.10 = (f32[64,256]{1,0:T(8,128)S(1)}, f32[64,256]{1,0:T(8,128)S(1)}, u32[]{:S(2)}, u32[]{:S(2)}) collective-permute-start(f32[64,256]{1,0:T(8,128)S(1)} %add.19.refs_0_), channel_id=1, source_target_pairs={{0,1},{1,0},{2,3},{3,2},{4,5},{5,4},{6,7},{7,6},{8,9},{9,8},{10,11... | collective-permute-start | bytes 196616 | tf_op jit(solution)/shard_map/ppermute | solution.py:19
  33.4 0.0 collective-permute-done.8.refs_1_
  33.4 0.0 copy-done
  33.4 1.0 %shard_map.51 = (bf16[128,384]{1,0:T(8,128)(2,1)S(1)}, f32[64,3072]{1,0:T(8,128)S(1)}) custom-call(f32[64,384]{1,0:T(8,128)S(1)} %add.18.refs_0_, f32[64,384]{1,0:T(8,128)S(1)} %collective-permute-done.8.refs_1_, f32[64,640]{1,0:T(8,128)S(1)} %copy-done, bf16[640,3072]{1,0:T(8,128)(2,1)S(1)} %get-tuple-element.11.refs_8_.refs_3_.hi, ...), custom_call_target="tpu_custom_call" | custom-call | flops 452984832 | bytes 1048576 | tf_op jit(solution)/shard_map/pallas_call | solution.py:142
  34.4 1.7 %collective-permute-done.10.refs_1_ = f32[64,256]{1,0:T(8,128)S(1)} collective-permute-done((f32[64,256]{1,0:T(8,128)S(1)}, f32[64,256]{1,0:T(8,128)S(1)}, u32[]{:S(2)}, u32[]{:S(2)}) %collective-permute-start.10) | collective-permute-done | bytes 65568 | tf_op jit(solution)/shard_map/ppermute | solution.py:19
  36.1 0.6 %shard_map.53 = (bf16[128,256]{1,0:T(8,128)(2,1)S(1)}, f32[4,8,3072]{2,1,0:T(8,128)S(1)}, f32[4,8,3072]{2,1,0:T(8,128)S(1)}) custom-call(f32[64,256]{1,0:T(8,128)S(1)} %add.19.refs_0_, f32[64,256]{1,0:T(8,128)S(1)} %collective-permute-done.10.refs_1_, f32[64,640]{1,0:T(8,128)S(1)} %copy-done, bf16[640,3072]{1,0:T(8,128)(2,1)S(1)} %get-tuple-element.11.refs_8_.refs_3_.hi, ...), custom_call_target="tpu_custom_call" | custom-call | flops 301989888 | bytes 1048576 | tf_op jit(solution)/shard_map/pallas_call | solution.py:142
  36.8 0.1 collective-permute-start.11
  36.9 1.7 %collective-permute-done.11 = f32[4,8,3072]{2,1,0:T(8,128)S(1)} collective-permute-done((f32[4,8,3072]{2,1,0:T(8,128)S(1)}, f32[4,8,3072]{2,1,0:T(8,128)S(1)}, u32[]{:S(2)}, u32[]{:S(2)}) %collective-permute-start.11) | collective-permute-done | bytes 393248 | tf_op jit(solution)/shard_map/ppermute | solution.py:19
  38.6 2.5 %collective-permute-start.14 = (f32[8,3072]{1,0:T(8,128)S(1)}, f32[8,3072]{1,0:T(8,128)S(1)}, u32[]{:S(2)}, u32[]{:S(2)}) collective-permute-start(f32[8,3072]{1,0:T(8,128)S(1)} %get-tuple-element.21), channel_id=1, source_target_pairs={{0,24},{4,28},{8,16},{12,20},{16,8},{20,12},{24,0},{28,4},{1,25},{... | collective-permute-start | bytes 294920 | tf_op jit(solution)/shard_map/ppermute | solution.py:19
  41.2 0.7 %collective-permute-start.13 = (f32[8,3072]{1,0:T(8,128)S(1)}, f32[8,3072]{1,0:T(8,128)S(1)}, u32[]{:S(2)}, u32[]{:S(2)}) collective-permute-start(f32[8,3072]{1,0:T(8,128)S(1)} %get-tuple-element.22), channel_id=1, source_target_pairs={{0,8},{4,12},{8,0},{12,4},{16,24},{20,28},{24,16},{28,20},{1,9},{5... | collective-permute-start | bytes 294920 | tf_op jit(solution)/shard_map/ppermute | solution.py:19
  41.9 1.2 %collective-permute-start.12 = (f32[8,3072]{1,0:T(8,128)S(1)}, f32[8,3072]{1,0:T(8,128)S(1)}, u32[]{:S(2)}, u32[]{:S(2)}) collective-permute-start(f32[8,3072]{1,0:T(8,128)S(1)} %get-tuple-element.20), channel_id=1, source_target_pairs={{0,16},{4,20},{8,24},{12,28},{16,0},{20,4},{24,8},{28,12},{1,17},{... | collective-permute-start | bytes 294920 | tf_op jit(solution)/shard_map/ppermute | solution.py:19
  43.1 4.7 %gradient_jb.1 = f32[640,3072]{1,0:T(8,128)} custom-call(bf16[128,384]{1,0:T(8,128)(2,1)S(1)} %get-tuple-element.14.one, bf16[128,256]{1,0:T(8,128)(2,1)S(1)} %get-tuple-element.17.two, bf16[128,3072]{1,0:T(8,128)(2,1)S(1)} %get-tuple-element.15.parts.ia), custom_call_target="tpu_custom_call" | custom-call | flops 754974720 | bytes 7864320 | tf_op jit(solution)/shard_map/gradient_jb/pallas_call | solution.py:164
  47.8 0.0 collective-permute-done.14
  47.8 0.6 %collective-permute-done.13 = f32[8,3072]{1,0:T(8,128)S(1)} collective-permute-done((f32[8,3072]{1,0:T(8,128)S(1)}, f32[8,3072]{1,0:T(8,128)S(1)}, u32[]{:S(2)}, u32[]{:S(2)}) %collective-permute-start.13) | collective-permute-done | bytes 98336 | tf_op jit(solution)/shard_map/ppermute | solution.py:19
  48.4 2.5 %collective-permute-done.12 = f32[8,3072]{1,0:T(8,128)S(1)} collective-permute-done((f32[8,3072]{1,0:T(8,128)S(1)}, f32[8,3072]{1,0:T(8,128)S(1)}, u32[]{:S(2)}, u32[]{:S(2)}) %collective-permute-start.12) | collective-permute-done | bytes 98336 | tf_op jit(solution)/shard_map/ppermute | solution.py:19
  50.9 0.7 %fusion.2 = f32[8,3072]{1,0:T(8,128)} fusion(f32[8,3072]{1,0:T(8,128)S(1)} %collective-permute-done.14, f32[8,3072]{1,0:T(8,128)S(1)} %collective-permute-done.13, f32[8,3072]{1,0:T(8,128)S(1)} %collective-permute-done.12, f32[4,8,3072]{2,1,0:T(8,128)S(1)} %add.20), kind=kLoop, calls=%fused_computation.6 | loop fusion | flops 73728 | bytes 491520 | tf_op jit(solution)/shard_map/add | solution.py:225
  (4 shorter events, 0.1 us)
Async XLA Ops:
  0.6 17.8 %copy-start.1 = (f32[8,3072]{1,0:T(8,128)S(1)}, f32[8,3072]{1,0:T(8,128)}, u32[]{:S(2)}) copy-start(f32[8,3072]{1,0:T(8,128)} %refs_0_.1) | copy-start | bytes 294916
  0.6 6.1 %collective-permute-start.1 = (f32[8,3072]{1,0:T(8,128)}, f32[8,3072]{1,0:T(8,128)S(1)}, u32[]{:S(2)}, u32[]{:S(2)}) collective-permute-start(f32[8,3072]{1,0:T(8,128)} %refs_0_.1), channel_id=1, source_target_pairs={{0,8},{4,12},{8,0},{12,4},{16,24},{20,28},{24,16},{28,20},{1,9},{5... | collective-permute-start | bytes 294920 | tf_op jit(solution)/shard_map/ppermute | solution.py:19
  3.8 10.6 %collective-permute-start.3 = (f32[8,3072]{1,0:T(8,128)}, f32[8,3072]{1,0:T(8,128)S(1)}, u32[]{:S(2)}, u32[]{:S(2)}) collective-permute-start(f32[8,3072]{1,0:T(8,128)} %refs_0_.1), channel_id=1, source_target_pairs={{0,16},{4,20},{8,24},{12,28},{16,0},{20,4},{24,8},{28,12},{1,17},{... | collective-permute-start | bytes 294920 | tf_op jit(solution)/shard_map/ppermute | solution.py:19
  6.3 8.1 %collective-permute-start.5 = (f32[8,3072]{1,0:T(8,128)}, f32[8,3072]{1,0:T(8,128)S(1)}, u32[]{:S(2)}, u32[]{:S(2)}) collective-permute-start(f32[8,3072]{1,0:T(8,128)} %refs_0_.1), channel_id=1, source_target_pairs={{0,24},{4,28},{8,16},{12,20},{16,8},{20,12},{24,0},{28,4},{1,25},{... | collective-permute-start | bytes 294920 | tf_op jit(solution)/shard_map/ppermute | solution.py:19
  6.3 12.1 %collective-permute-start = (f32[8,3072]{1,0:T(8,128)}, f32[8,3072]{1,0:T(8,128)S(1)}, u32[]{:S(2)}, u32[]{:S(2)}) collective-permute-start(f32[8,3072]{1,0:T(8,128)} %refs_0_.1), channel_id=1, source_target_pairs={{0,4},{4,0},{8,12},{12,8},{16,20},{20,16},{24,28},{28,24},{1,5},{5... | collective-permute-start | bytes 294920 | tf_op jit(solution)/shard_map/ppermute | solution.py:19
  6.8 11.7 %collective-permute-start.2 = (f32[8,3072]{1,0:T(8,128)S(1)}, f32[8,3072]{1,0:T(8,128)S(1)}, u32[]{:S(2)}, u32[]{:S(2)}) collective-permute-start(f32[8,3072]{1,0:T(8,128)S(1)} %collective-permute-done.1.refs_2_), channel_id=1, source_target_pairs={{0,4},{4,0},{8,12},{12,8},{16,20},{20,16},{24,28},{28,24},{1,5},{5... | collective-permute-start | bytes 294920 | tf_op jit(solution)/shard_map/ppermute | solution.py:19
  14.4 4.0 %collective-permute-start.4 = (f32[8,3072]{1,0:T(8,128)S(1)}, f32[8,3072]{1,0:T(8,128)S(1)}, u32[]{:S(2)}, u32[]{:S(2)}) collective-permute-start(f32[8,3072]{1,0:T(8,128)S(1)} %collective-permute-done.3.refs_4_), channel_id=1, source_target_pairs={{0,4},{4,0},{8,12},{12,8},{16,20},{20,16},{24,28},{28,24},{1,5},{5... | collective-permute-start | bytes 294920 | tf_op jit(solution)/shard_map/ppermute | solution.py:19
  14.4 4.0 %collective-permute-start.6 = (f32[8,3072]{1,0:T(8,128)S(1)}, f32[8,3072]{1,0:T(8,128)S(1)}, u32[]{:S(2)}, u32[]{:S(2)}) collective-permute-start(f32[8,3072]{1,0:T(8,128)S(1)} %collective-permute-done.5.refs_6_), channel_id=1, source_target_pairs={{0,4},{4,0},{8,12},{12,8},{16,20},{20,16},{24,28},{28,24},{1,5},{5... | collective-permute-start | bytes 294920 | tf_op jit(solution)/shard_map/ppermute | solution.py:19
  18.5 14.9 %copy-start = (f32[64,640]{1,0:T(8,128)S(1)}, f32[64,640]{1,0:T(8,128)}, u32[]{:S(2)}) copy-start(f32[64,640]{1,0:T(8,128)} %refs_2_.3) | copy-start | bytes 491524
  20.0 4.8 %collective-permute-start.7 = (f32[64,384]{1,0:T(8,128)S(1)}, f32[64,384]{1,0:T(8,128)S(1)}, u32[]{:S(2)}, u32[]{:S(2)}) collective-permute-start(f32[64,384]{1,0:T(8,128)S(1)} %get-tuple-element.13), channel_id=1, source_target_pairs={{0,1},{1,0},{2,3},{3,2},{4,5},{5,4},{6,7},{7,6},{8,9},{9,8},{10,11... | collective-permute-start | bytes 294920 | tf_op jit(solution)/shard_map/ppermute | solution.py:19
  24.8 8.6 %collective-permute-start.8 = (f32[64,384]{1,0:T(8,128)S(1)}, f32[64,384]{1,0:T(8,128)S(1)}, u32[]{:S(2)}, u32[]{:S(2)}) collective-permute-start(f32[64,384]{1,0:T(8,128)S(1)} %add.18.refs_0_), channel_id=1, source_target_pairs={{0,2},{1,3},{2,0},{3,1},{4,6},{5,7},{6,4},{7,5},{8,10},{9,11},{10,... | collective-permute-start | bytes 294920 | tf_op jit(solution)/shard_map/ppermute | solution.py:19
  27.5 4.3 %collective-permute-start.9 = (f32[64,256]{1,0:T(8,128)S(1)}, f32[64,256]{1,0:T(8,128)S(1)}, u32[]{:S(2)}, u32[]{:S(2)}) collective-permute-start(f32[64,256]{1,0:T(8,128)S(1)} %shard_map.52), channel_id=1, source_target_pairs={{0,2},{1,3},{2,0},{3,1},{4,6},{5,7},{6,4},{7,5},{8,10},{9,11},{10,... | collective-permute-start | bytes 196616 | tf_op jit(solution)/shard_map/ppermute | solution.py:19
  31.8 4.3 %collective-permute-start.10 = (f32[64,256]{1,0:T(8,128)S(1)}, f32[64,256]{1,0:T(8,128)S(1)}, u32[]{:S(2)}, u32[]{:S(2)}) collective-permute-start(f32[64,256]{1,0:T(8,128)S(1)} %add.19.refs_0_), channel_id=1, source_target_pairs={{0,1},{1,0},{2,3},{3,2},{4,5},{5,4},{6,7},{7,6},{8,9},{9,8},{10,11... | collective-permute-start | bytes 196616 | tf_op jit(solution)/shard_map/ppermute | solution.py:19
  36.8 1.8 %collective-permute-start.11 = (f32[4,8,3072]{2,1,0:T(8,128)S(1)}, f32[4,8,3072]{2,1,0:T(8,128)S(1)}, u32[]{:S(2)}, u32[]{:S(2)}) collective-permute-start(f32[4,8,3072]{2,1,0:T(8,128)S(1)} %get-tuple-element.19), channel_id=1, source_target_pairs={{0,4},{4,0},{8,12},{12,8},{16,20},{20,16},{24,28},{28,24},{1,5},{5... | collective-permute-start | bytes 1179656 | tf_op jit(solution)/shard_map/ppermute | solution.py:19
  38.6 9.2 %collective-permute-start.14 = (f32[8,3072]{1,0:T(8,128)S(1)}, f32[8,3072]{1,0:T(8,128)S(1)}, u32[]{:S(2)}, u32[]{:S(2)}) collective-permute-start(f32[8,3072]{1,0:T(8,128)S(1)} %get-tuple-element.21), channel_id=1, source_target_pairs={{0,24},{4,28},{8,16},{12,20},{16,8},{20,12},{24,0},{28,4},{1,25},{... | collective-permute-start | bytes 294920 | tf_op jit(solution)/shard_map/ppermute | solution.py:19
  41.2 7.3 %collective-permute-start.13 = (f32[8,3072]{1,0:T(8,128)S(1)}, f32[8,3072]{1,0:T(8,128)S(1)}, u32[]{:S(2)}, u32[]{:S(2)}) collective-permute-start(f32[8,3072]{1,0:T(8,128)S(1)} %get-tuple-element.22), channel_id=1, source_target_pairs={{0,8},{4,12},{8,0},{12,4},{16,24},{20,28},{24,16},{28,20},{1,9},{5... | collective-permute-start | bytes 294920 | tf_op jit(solution)/shard_map/ppermute | solution.py:19
  41.9 9.0 %collective-permute-start.12 = (f32[8,3072]{1,0:T(8,128)S(1)}, f32[8,3072]{1,0:T(8,128)S(1)}, u32[]{:S(2)}, u32[]{:S(2)}) collective-permute-start(f32[8,3072]{1,0:T(8,128)S(1)} %get-tuple-element.20), channel_id=1, source_target_pairs={{0,16},{4,20},{8,24},{12,28},{16,0},{20,4},{24,8},{28,12},{1,17},{... | collective-permute-start | bytes 294920 | tf_op jit(solution)/shard_map/ppermute | solution.py:19

commit v3 on v1

v3 whole, which is shorter than its diff:
```python
import jax
import jax.numpy as jnp
from jax import lax
from jax.experimental import pallas as pl
from jax.experimental.pallas import tpu as pltpu
from jax.sharding import PartitionSpec as P


F32, BF16 = jnp.float32, jnp.bfloat16
VMEM = pl.BlockSpec(memory_space=pltpu.VMEM)
HBM = pl.BlockSpec(memory_space=pltpu.HBM)
MIB = 1 << 20


def swap(x, axis, distance):
    size = lax.axis_size(axis)
    return lax.ppermute(x, axis, [(i, i ^ distance) for i in range(size)])


def split(x):
    hi = x.astype(BF16)
    return hi, (x - hi.astype(F32)).astype(BF16)


def mxu(a, b, dims):
    return lax.dot_general(a, b, (dims, ((), ())), preferred_element_type=F32)


def width_of(size, most):
    fits = [w for w in range(128, min(size, most) + 1, 128) if size % w == 0]
    return fits[-1] if fits else size


def prepare(factor_jb):
    height, width = factor_jb.shape
    piece = width_of(height, 128)
    pieces = height // piece
    step = width_of(width, 1024)

    def kernel(jb, hi, lo, hi_t, lo_t, held, sems):
        def copy(p):
            at = pl.ds(p * piece, piece)
            return pltpu.make_async_copy(jb.at[at], held.at[at], sems.at[p])

        for p in range(pieces):
            copy(p).start()
        for p in range(pieces):
            copy(p).wait()
            rows = pl.ds(p * piece, piece)

            @pl.loop(0, width // step)
            def _(c, rows=rows):
                columns = pl.ds(pl.multiple_of(c * step, step), step)
                a, b = split(held[rows, columns])
                hi[rows, columns], lo[rows, columns] = a, b
                hi_t[columns, rows], lo_t[columns, rows] = a.T, b.T

    plain = jax.ShapeDtypeStruct((height, width), BF16)
    turned = jax.ShapeDtypeStruct((width, height), BF16)
    return pl.pallas_call(
        kernel,
        name="prepare",
        out_shape=(plain, plain, turned, turned),
        in_specs=[HBM],
        out_specs=(VMEM,) * 4,
        scratch_shapes=[pltpu.VMEM((height, width), F32), pltpu.SemaphoreType.DMA((pieces,))],
        compiler_params=pltpu.CompilerParams(vmem_limit_bytes=38 * MIB),
        cost_estimate=pl.CostEstimate(flops=4 * height * width, bytes_accessed=4 * height * width, transcendentals=0),
    )(factor_jb)


def integral_share(blocks, hi_t, lo_t):
    n = len(blocks)
    height, width = blocks[0].shape
    rows = n * height
    columns = hi_t.shape[1]
    tile = width_of(columns, 128)

    def kernel(*refs):
        block_refs, (hi, lo, out, parts) = refs[:n], refs[n:]
        for pair in range(n // 2):
            x = jnp.concatenate([block_refs[2 * pair][...], block_refs[2 * pair + 1][...]])
            a, b = split(x)
            at = 2 * height * pair
            parts[pl.ds(at, 2 * height)] = a
            parts[pl.ds(rows + at, 2 * height)] = b
        for t in range(columns // tile):
            at = pl.ds(t * tile, tile)
            both = mxu(parts[...], hi[:, at], ((1,), (0,)))
            rest = mxu(parts[pl.ds(0, rows)], lo[:, at], ((1,), (0,)))
            out[:, at] = both[:rows] + (both[rows:] + rest)

    return pl.pallas_call(
        kernel,
        out_shape=(jax.ShapeDtypeStruct((rows, columns), F32), jax.ShapeDtypeStruct((2 * rows, width), BF16)),
        in_specs=[VMEM] * (n + 2),
        out_specs=(VMEM, VMEM),
        compiler_params=pltpu.CompilerParams(vmem_limit_bytes=20 * MIB),
        cost_estimate=pl.CostEstimate(flops=6 * rows * width * columns, bytes_accessed=MIB, transcendentals=0),
    )(*blocks, hi_t, lo_t)


def gradient_share(mine, theirs, denominators, jb_hi, jb_lo, distances, height):
    rows, columns = mine.shape
    width = jb_hi.shape[1]
    n = len(distances)
    tile = width_of(width, 512)

    def kernel(mine, theirs, denom, hi, lo, parts, *rest):
        outs, amp = rest[:n], rest[n]
        me = lax.axis_index("row")
        for slot, d in enumerate(distances):
            at = pl.multiple_of((me ^ d) * height, height)
            here = pl.ds(slot * height, height)
            amp[here] = (mine[here] + theirs[here]) / denom[pl.ds(at, height)]
        a, b = split(amp[...])
        parts[pl.ds(0, rows)] = a
        parts[pl.ds(rows, rows)] = b
        for t in range(width // tile):
            at = pl.ds(t * tile, tile)
            both = mxu(parts[...], hi[:, at], ((1,), (0,)))
            rest = mxu(parts[pl.ds(0, rows)], lo[:, at], ((1,), (0,)))
            total = both[:rows] + (both[rows:] + rest)
            for slot in range(n):
                outs[slot][:, at] = total[slot * height : (slot + 1) * height]

    block = jax.ShapeDtypeStruct((height, width), F32)
    amp, *outs = pl.pallas_call(
        kernel,
        out_shape=(jax.ShapeDtypeStruct((2 * rows, columns), BF16),) + (block,) * n,
        in_specs=[VMEM] * 5,
        out_specs=(VMEM,) * (1 + n),
        scratch_shapes=[pltpu.VMEM((rows, columns), F32)],
        compiler_params=pltpu.CompilerParams(vmem_limit_bytes=20 * MIB),
        cost_estimate=pl.CostEstimate(flops=6 * rows * width * columns, bytes_accessed=MIB, transcendentals=0),
    )(mine, theirs, denominators, jb_hi, jb_lo)
    return amp, dict(zip(distances, outs))


def gradient_jb(amp_parts, ia_parts):
    n = len(amp_parts)
    width, columns = ia_parts[0].shape[1], amp_parts[0].shape[1]
    deep = 3 * sum(i.shape[0] for i in ia_parts) // 2
    tile = width_of(width, 512)
    tiles = width // tile

    def kernel(*refs):
        amps, ias, (out, left, held, sems) = refs[:n], refs[n : 2 * n], refs[2 * n :]
        pieces = []
        for amp in amps:
            rows = amp.shape[0] // 2
            hi, lo = amp[pl.ds(0, rows)].astype(F32), amp[pl.ds(rows, rows)].astype(F32)
            pieces += [hi, lo, hi]
        left[...] = jnp.concatenate(pieces).T.astype(BF16)
        copies = []
        for t in range(tiles):
            here = pl.ds(t * tile, tile)
            pieces = []
            for ia in ias:
                rows = ia.shape[0] // 2
                hi, lo = ia[pl.ds(0, rows), here], ia[pl.ds(rows, rows), here]
                pieces += [hi, hi, lo]
            held[t] = mxu(left[...], jnp.concatenate(pieces), ((1,), (0,)))
            copies.append(pltpu.make_async_copy(held.at[t], out.at[:, here], sems.at[t]))
            copies[-1].start()
        for copy in copies:
            copy.wait()

    return pl.pallas_call(
        kernel,
        name="gradient_jb",
        out_shape=jax.ShapeDtypeStruct((columns, width), F32),
        in_specs=[VMEM] * (2 * n),
        out_specs=HBM,
        scratch_shapes=[
            pltpu.VMEM((columns, deep), BF16),
            pltpu.VMEM((tiles, columns, tile), F32),
            pltpu.SemaphoreType.DMA((tiles,)),
        ],
        compiler_params=pltpu.CompilerParams(vmem_limit_bytes=20 * MIB),
        cost_estimate=pl.CostEstimate(
            flops=2 * deep * width * columns, bytes_accessed=4 * width * columns, transcendentals=0
        ),
    )(*amp_parts, *ia_parts)


def chunks_of(rows):
    chips = range(1, rows // 2)
    last = [k for k in chips if k % 4 == 3]
    return [[*sorted(set(chips) - set(last), reverse=True), 0], last]


def aux_steps(aux):
    return aux.bit_length() - 1


def exchange(x, step):
    rows, aux = lax.axis_size("row"), lax.axis_size("aux")
    steps = aux_steps(aux)

    def partner(row, column):
        bit = (step + row % 2 * (steps // 2)) % steps
        return row * aux + (column ^ 1 << bit)

    pairs = [(row * aux + column, partner(row, column)) for row in range(rows) for column in range(aux)]
    return lax.ppermute(x, ("row", "aux"), pairs)


def per_device(factor_ia, factor_jb, denominators):
    rows = lax.axis_size("row")
    aux = lax.axis_size("aux")
    height = factor_ia.shape[0]

    blocks = {0: factor_ia}
    for k in range(1, rows // 2):
        blocks[2 * k] = swap(factor_ia, "row", 2 * k)
    for d in range(0, rows, 2):
        blocks[d + 1] = swap(blocks[d], "row", 1)
    jb_hi, jb_lo, hi_t, lo_t = prepare(factor_jb)

    amp_parts, ia_parts, sums = [], [], []
    for ks in chunks_of(rows):
        distances = [d for k in ks for d in (2 * k, 2 * k + 1)]
        share, ia = integral_share([blocks[d] for d in distances], hi_t, lo_t)
        for step in range(aux_steps(aux) - 1):
            share = share + exchange(share, step)
        theirs = exchange(share, aux_steps(aux) - 1)
        amp, outs = gradient_share(share, theirs, denominators, jb_hi, jb_lo, distances, height)
        for k in ks:
            folded = outs[2 * k] + swap(outs[2 * k + 1], "row", 1)
            sums.append(swap(folded, "row", 2 * k) if k else folded)
        amp_parts.append(amp)
        ia_parts.append(ia)

    grad_ia = sums[0]
    for part in sums[1:]:
        grad_ia = grad_ia + part
    grad_jb = gradient_jb(amp_parts, ia_parts)
    return (grad_jb, grad_ia)


def solution(mesh):
    return jax.shard_map(
        per_device,
        mesh=mesh,
        in_specs=(P("row", "aux"), P("row", "aux"), P(None, "row")),
        out_specs=(P("row", "aux"), P("row", "aux")),
        check_vma=False,
    )
```

time: 58.6 us -> 51.3 us (0.88)
  matrix products: 18.2 us -> 0 us
  Pallas kernels: 0 us -> 13.8 us
  starting transfers between devices: 13.4 us -> 18.8 us
  waiting for transfers between devices: 21.1 us -> 17 us
  local copies, waits for them, and re-layouts: 2.99 us -> 0.01 us
  other arithmetic: 1.73 us -> 0.74 us
    dot_general x3 -> x0, matrix products: 18.2 us -> none  [dot(): lax.dot_general(a, b, (dims, ((), ())), precision=HIGH, preferred_element...]
    pallas_call x0 -> x6, Pallas kernels: none -> 13.8 us  [the longest x1 4.91 us: prepare(): pl.pallas_call(kernel, name='prepare', out_shape=(plain, plain, turned, t...]
    ppermute x10 -> x14, waiting for transfers between devices: 21.1 us -> 7.6 us  [swap(): return lax.ppermute(x, axis, [(i, i ^ distance) for i in range(size)])]
    ppermute x0 -> x4, waiting for transfers between devices: none -> 9.39 us  [exchange(): return lax.ppermute(x, ('row', 'aux'), pairs)]
    ppermute x0 -> x4, starting transfers between devices: none -> 5.2 us  [exchange(): return lax.ppermute(x, ('row', 'aux'), pairs)]
    unnamed x9 -> x4, local copies, waits for them, and re-layouts: 2.94 us -> 0.01 us
    another operation x2 -> x0, other arithmetic: 1 us -> none  [per_device(): whole_ia = jnp.stack([even, odd], axis=1).reshape(rows * height, -1)]
    ppermute x10 -> x14, starting transfers between devices: 13.4 us -> 13.6 us  [swap(): return lax.ppermute(x, axis, [(i, i ^ distance) for i in range(size)])]
  transfers between devices with their start and end apart: 10 -> 18, of which waited for: 7 -> 6; matrix products, arithmetic and copies ran while one was open for 14% -> 0% of each run, Pallas kernels for 0% -> 27%
where the time goes in v3:
time: 51.3 us; the launch traced here: 51.1 us
  starting transfers between devices  18.8 us (37%)
  waiting for transfers between devices  17 us (33%)
  Pallas kernels  13.8 us (27%)
  between operations  0.77 us (2%)
  other arithmetic  0.74 us (1%)
    ppermute x14, starting transfers between devices, swap(): return lax.ppermute(x, axis, [(i, i ^ distance) for i in range(size)])  13.6 us
    ppermute x4, waiting for transfers between devices, exchange(): return lax.ppermute(x, ('row', 'aux'), pairs)  9.39 us
    ppermute x14, waiting for transfers between devices, swap(): return lax.ppermute(x, axis, [(i, i ^ distance) for i in range(size)])  7.6 us
    ppermute x4, starting transfers between devices, exchange(): return lax.ppermute(x, ('row', 'aux'), pairs)  5.2 us
    pallas_call x1, Pallas kernels, prepare(): pl.pallas_call(kernel, name='prepare', out_shape=(plain, plain, turned, t...  4.91 us
    pallas_call x1, Pallas kernels, gradient_jb(): pl.pallas_call(kernel, name='gradient_jb', out_shape=jax.ShapeDtypeStruct...  3.66 us
    pallas_call x2, Pallas kernels, gradient_share(): pl.pallas_call(kernel, out_shape=(jax.ShapeDtypeStruct((2 * rows, columns...  2.64 us
    pallas_call x2, Pallas kernels, integral_share(): pl.pallas_call(kernel, out_shape=(jax.ShapeDtypeStruct((rows, columns), F...  2.61 us
  transfers between devices with their start and end apart: 18, of which 6 were waited for; matrix products, arithmetic and copies ran while one was open for 0% of the time, Pallas kernels for 27%

profile of v3, /device:TPU:0, one launch (start us, length us, event | category | flops | bytes accessed | tf_op | source)
XLA Modules:
  0.0 51.1 jit_solution(15090418407841881750)
XLA Ops:
  0.6 0.0 copy-start.1
  0.6 3.1 %collective-permute-start.2 = (f32[8,3072]{1,0:T(8,128)}, f32[8,3072]{1,0:T(8,128)S(1)}, u32[]{:S(2)}, u32[]{:S(2)}) collective-permute-start(f32[8,3072]{1,0:T(8,128)} %refs_4_.1), channel_id=1, source_target_pairs={{0,8},{4,12},{8,0},{12,4},{16,24},{20,28},{24,16},{28,20},{1,9},{5... | collective-permute-start | bytes 294920 | tf_op jit(solution)/shard_map/ppermute | solution.py:17
  3.8 2.6 %collective-permute-start = (f32[8,3072]{1,0:T(8,128)}, f32[8,3072]{1,0:T(8,128)S(1)}, u32[]{:S(2)}, u32[]{:S(2)}) collective-permute-start(f32[8,3072]{1,0:T(8,128)} %refs_4_.1), channel_id=1, source_target_pairs={{0,16},{4,20},{8,24},{12,28},{16,0},{20,4},{24,8},{28,12},{1,17},{... | collective-permute-start | bytes 294920 | tf_op jit(solution)/shard_map/ppermute | solution.py:17
  6.3 0.0 collective-permute-start.4
  6.3 0.4 collective-permute-done.2.refs_2_
  6.8 0.1 collective-permute-start.3
  6.9 4.4 %collective-permute-done.refs_0_ = f32[8,3072]{1,0:T(8,128)S(1)} collective-permute-done((f32[8,3072]{1,0:T(8,128)}, f32[8,3072]{1,0:T(8,128)S(1)}, u32[]{:S(2)}, u32[]{:S(2)}) %collective-permute-start) | collective-permute-done | bytes 98336 | tf_op jit(solution)/shard_map/ppermute | solution.py:17
  11.3 0.0 collective-permute-start.1
  11.3 2.4 %collective-permute-start.7 = (f32[8,3072]{1,0:T(8,128)}, f32[8,3072]{1,0:T(8,128)S(1)}, u32[]{:S(2)}, u32[]{:S(2)}) collective-permute-start(f32[8,3072]{1,0:T(8,128)} %refs_4_.1), channel_id=1, source_target_pairs={{0,24},{4,28},{8,16},{12,20},{16,8},{20,12},{24,0},{28,4},{1,25},{... | collective-permute-start | bytes 294920 | tf_op jit(solution)/shard_map/ppermute | solution.py:17
  13.7 4.9 %prepare.1 = (bf16[640,3072]{1,0:T(8,128)(2,1)S(1)}, bf16[640,3072]{1,0:T(8,128)(2,1)S(1)}, bf16[3072,640]{1,0:T(8,128)(2,1)S(1)}, bf16[3072,640]{1,0:T(8,128)(2,1)S(1)}) custom-call(f32[640,3072]{1,0:T(8,128)} %jb.1), custom_call_target="tpu_custom_call" | custom-call | flops 7864320 | bytes 7864320 | tf_op jit(solution)/shard_map/prepare/pallas_call | solution.py:60
  18.6 0.0 collective-permute-done.4.refs_5_
  18.6 0.0 collective-permute-done.3.refs_3_
  18.6 0.0 collective-permute-done.1.refs_1_
  18.7 0.0 copy-done.1
  18.7 1.4 %shard_map.50 = (f32[48,640]{1,0:T(8,128)S(1)}, bf16[96,3072]{1,0:T(8,128)(2,1)S(1)}) custom-call(f32[8,3072]{1,0:T(8,128)S(1)} %collective-permute-done.refs_0_, f32[8,3072]{1,0:T(8,128)S(1)} %collective-permute-done.1.refs_1_, f32[8,3072]{1,0:T(8,128)S(1)} %collective-permute-done.2.refs_2_, f32[8,3072]{1,0:T(8,128)S(1)} %collective-permute-done.3.refs_3_, ...), custom_call_target="tpu_custom_call" | custom-call | flops 566231040 | bytes 1048576 | tf_op jit(solution)/shard_map/pallas_call | solution.py:93
  20.1 1.6 %collective-permute-start.5 = (f32[48,640]{1,0:T(8,128)S(1)}, f32[48,640]{1,0:T(8,128)S(1)}, u32[]{:S(2)}, u32[]{:S(2)}) collective-permute-start(f32[48,640]{1,0:T(8,128)S(1)} %get-tuple-element.22), channel_id=1, source_target_pairs={{0,1},{1,0},{2,3},{3,2},{4,6},{5,7},{6,4},{7,5},{8,9},{9,8},{10,11... | collective-permute-start | bytes 368648 | tf_op jit(solution)/shard_map/ppermute | solution.py:206
  21.7 0.0 collective-permute-done.7.refs_0_
  21.7 0.0 collective-permute-start.8
  21.7 3.4 %collective-permute-done.5 = f32[48,640]{1,0:T(8,128)S(1)} collective-permute-done((f32[48,640]{1,0:T(8,128)S(1)}, f32[48,640]{1,0:T(8,128)S(1)}, u32[]{:S(2)}, u32[]{:S(2)}) %collective-permute-start.5) | collective-permute-done | bytes 122912 | tf_op jit(solution)/shard_map/ppermute | solution.py:206
  25.1 0.0 copy-start
  25.1 1.6 %collective-permute-start.6 = (f32[48,640]{1,0:T(8,128)S(1)}, f32[48,640]{1,0:T(8,128)S(1)}, u32[]{:S(2)}, u32[]{:S(2)}) collective-permute-start(f32[48,640]{1,0:T(8,128)S(1)} %add.27.mine), channel_id=1, source_target_pairs={{0,2},{1,3},{2,0},{3,1},{4,5},{5,4},{6,7},{7,6},{8,10},{9,11},{10,... | collective-permute-start | bytes 368648 | tf_op jit(solution)/shard_map/ppermute | solution.py:206
  26.7 0.0 collective-permute-done.8.refs_1_
  26.7 1.2 %shard_map.52 = (f32[16,640]{1,0:T(8,128)S(1)}, bf16[32,3072]{1,0:T(8,128)(2,1)S(1)}) custom-call(f32[8,3072]{1,0:T(8,128)S(1)} %collective-permute-done.7.refs_0_, f32[8,3072]{1,0:T(8,128)S(1)} %collective-permute-done.8.refs_1_, bf16[3072,640]{1,0:T(8,128)(2,1)S(1)} %get-tuple-element.20.refs_6_.refs_2_, ...), custom_call_target="tpu_custom_call" | custom-call | flops 188743680 | bytes 1048576 | tf_op jit(solution)/shard_map/pallas_call | solution.py:93
  27.8 1.6 %collective-permute-start.9 = (f32[16,640]{1,0:T(8,128)S(1)}, f32[16,640]{1,0:T(8,128)S(1)}, u32[]{:S(2)}, u32[]{:S(2)}) collective-permute-start(f32[16,640]{1,0:T(8,128)S(1)} %get-tuple-element.26), channel_id=1, source_target_pairs={{0,1},{1,0},{2,3},{3,2},{4,6},{5,7},{6,4},{7,5},{8,9},{9,8},{10,11... | collective-permute-start | bytes 122888 | tf_op jit(solution)/shard_map/ppermute | solution.py:206
  29.4 2.5 %collective-permute-done.9 = f32[16,640]{1,0:T(8,128)S(1)} collective-permute-done((f32[16,640]{1,0:T(8,128)S(1)}, f32[16,640]{1,0:T(8,128)S(1)}, u32[]{:S(2)}, u32[]{:S(2)}) %collective-permute-start.9) | collective-permute-done | bytes 40992 | tf_op jit(solution)/shard_map/ppermute | solution.py:206
  31.9 0.5 collective-permute-start.10
  32.4 3.5 %collective-permute-done.10.theirs = f32[16,640]{1,0:T(8,128)S(1)} collective-permute-done((f32[16,640]{1,0:T(8,128)S(1)}, f32[16,640]{1,0:T(8,128)S(1)}, u32[]{:S(2)}, u32[]{:S(2)}) %collective-permute-start.10) | collective-permute-done | bytes 40992 | tf_op jit(solution)/shard_map/ppermute | solution.py:206
  35.9 0.0 copy-done
  35.9 1.2 %shard_map.53 = (bf16[32,640]{1,0:T(8,128)(2,1)S(1)}, f32[8,3072]{1,0:T(8,128)S(1)}, f32[8,3072]{1,0:T(8,128)S(1)}) custom-call(f32[16,640]{1,0:T(8,128)S(1)} %add.28.mine, f32[16,640]{1,0:T(8,128)S(1)} %collective-permute-done.10.theirs, f32[64,640]{1,0:T(8,128)S(1)} %copy-done, bf16[640,3072]{1,0:T(8,128)(2,1)S(1)} %get-tuple-element.23.hi, ...), custom_call_target="tpu_custom_call" | custom-call | flops 188743680 | bytes 1048576 | tf_op jit(solution)/shard_map/pallas_call | solution.py:128
  37.1 0.0 collective-permute-start.16
  37.1 0.0 collective-permute-done.6.theirs
  37.2 1.4 %shard_map.51 = (bf16[96,640]{1,0:T(8,128)(2,1)S(1)}, f32[8,3072]{1,0:T(8,128)S(1)}, f32[8,3072]{1,0:T(8,128)S(1)}, f32[8,3072]{1,0:T(8,128)S(1)}, f32[8,3072]{1...) custom-call(f32[48,640]{1,0:T(8,128)S(1)} %add.27.mine, f32[48,640]{1,0:T(8,128)S(1)} %collective-permute-done.6.theirs, ...), custom_call_target="tpu_custom_call" | custom-call | flops 566231040 | bytes 1048576 | tf_op jit(solution)/shard_map/pallas_call | solution.py:128
  38.6 0.6 %collective-permute-start.11 = (f32[8,3072]{1,0:T(8,128)S(1)}, f32[8,3072]{1,0:T(8,128)S(1)}, u32[]{:S(2)}, u32[]{:S(2)}) collective-permute-start(f32[8,3072]{1,0:T(8,128)S(1)} %get-tuple-element.31), channel_id=1, source_target_pairs={{0,4},{4,0},{8,12},{12,8},{16,20},{20,16},{24,28},{28,24},{1,5},{5... | collective-permute-start | bytes 294920 | tf_op jit(solution)/shard_map/ppermute | solution.py:17
  39.1 0.1 collective-permute-start.13
  39.2 0.0 collective-permute-done.16
  39.2 1.5 %collective-permute-start.17 = (f32[8,3072]{1,0:T(8,128)S(1)}, f32[8,3072]{1,0:T(8,128)S(1)}, u32[]{:S(2)}, u32[]{:S(2)}) collective-permute-start(f32[8,3072]{1,0:T(8,128)S(1)} %add.34), channel_id=1, source_target_pairs={{0,24},{4,28},{8,16},{12,20},{16,8},{20,12},{24,0},{28,4},{1,25},{... | collective-permute-start | bytes 294920 | tf_op jit(solution)/shard_map/ppermute | solution.py:17
  40.7 0.2 collective-permute-start.15
  40.9 0.0 collective-permute-done.11
  40.9 0.1 collective-permute-start.12
  41.0 0.0 collective-permute-done.13
  41.0 3.0 %collective-permute-start.14 = (f32[8,3072]{1,0:T(8,128)S(1)}, f32[8,3072]{1,0:T(8,128)S(1)}, u32[]{:S(2)}, u32[]{:S(2)}) collective-permute-start(f32[8,3072]{1,0:T(8,128)S(1)} %add.30), channel_id=1, source_target_pairs={{0,8},{4,12},{8,0},{12,4},{16,24},{20,28},{24,16},{28,20},{1,9},{5... | collective-permute-start | bytes 294920 | tf_op jit(solution)/shard_map/ppermute | solution.py:17
  44.0 3.7 %gradient_jb.1 = f32[640,3072]{1,0:T(8,128)} custom-call(bf16[96,640]{1,0:T(8,128)(2,1)S(1)} %get-tuple-element.25.refs_0_, bf16[32,640]{1,0:T(8,128)(2,1)S(1)} %get-tuple-element.27.refs_1_, bf16[96,3072]{1,0:T(8,128)(2,1)S(1)} %get-tuple-element.28.refs_2_, bf16[32,3072]{1,0:T(8,128)(2,1)S(1)} %get-tuple-element.29.refs_3_), custom_call_target="tpu_custom_call" | custom-call | flops 754974720 | bytes 7864320 | tf_op jit(solution)/shard_map/gradient_jb/pallas_call | solution.py:169
  47.7 0.0 collective-permute-done.17
  47.7 0.0 collective-permute-done.15
  47.7 2.7 %collective-permute-done.12 = f32[8,3072]{1,0:T(8,128)S(1)} collective-permute-done((f32[8,3072]{1,0:T(8,128)S(1)}, f32[8,3072]{1,0:T(8,128)S(1)}, u32[]{:S(2)}, u32[]{:S(2)}) %collective-permute-start.12) | collective-permute-done | bytes 98336 | tf_op jit(solution)/shard_map/ppermute | solution.py:17
  50.5 0.0 collective-permute-done.14
  50.5 0.7 %add_add_fusion = f32[8,3072]{1,0:T(8,128)} fusion(f32[8,3072]{1,0:T(8,128)S(1)} %collective-permute-done.17, f32[8,3072]{1,0:T(8,128)S(1)} %get-tuple-element.34, f32[8,3072]{1,0:T(8,128)S(1)} %collective-permute-done.15, f32[8,3072]{1,0:T(8,128)S(1)} %collective-permute-done.12, f32[8,3072]{1,0:T(8,128)S(1)} %collective-permute-done.14), kind=kLoop, calls=%fused_computation | loop fusion | flops 98304 | bytes 589824 | tf_op jit(solution)/shard_map/add | solution.py:237
  (5 shorter events, 0.1 us)
Async XLA Ops:
  0.6 18.0 %copy-start.1 = (f32[8,3072]{1,0:T(8,128)S(1)}, f32[8,3072]{1,0:T(8,128)}, u32[]{:S(2)}) copy-start(f32[8,3072]{1,0:T(8,128)} %refs_4_.1) | copy-start | bytes 294916
  0.6 6.1 %collective-permute-start.2 = (f32[8,3072]{1,0:T(8,128)}, f32[8,3072]{1,0:T(8,128)S(1)}, u32[]{:S(2)}, u32[]{:S(2)}) collective-permute-start(f32[8,3072]{1,0:T(8,128)} %refs_4_.1), channel_id=1, source_target_pairs={{0,8},{4,12},{8,0},{12,4},{16,24},{20,28},{24,16},{28,20},{1,9},{5... | collective-permute-start | bytes 294920 | tf_op jit(solution)/shard_map/ppermute | solution.py:17
  3.8 7.5 %collective-permute-start = (f32[8,3072]{1,0:T(8,128)}, f32[8,3072]{1,0:T(8,128)S(1)}, u32[]{:S(2)}, u32[]{:S(2)}) collective-permute-start(f32[8,3072]{1,0:T(8,128)} %refs_4_.1), channel_id=1, source_target_pairs={{0,16},{4,20},{8,24},{12,28},{16,0},{20,4},{24,8},{28,12},{1,17},{... | collective-permute-start | bytes 294920 | tf_op jit(solution)/shard_map/ppermute | solution.py:17
  6.3 12.3 %collective-permute-start.4 = (f32[8,3072]{1,0:T(8,128)}, f32[8,3072]{1,0:T(8,128)S(1)}, u32[]{:S(2)}, u32[]{:S(2)}) collective-permute-start(f32[8,3072]{1,0:T(8,128)} %refs_4_.1), channel_id=1, source_target_pairs={{0,4},{4,0},{8,12},{12,8},{16,20},{20,16},{24,28},{28,24},{1,5},{5... | collective-permute-start | bytes 294920 | tf_op jit(solution)/shard_map/ppermute | solution.py:17
  6.8 11.9 %collective-permute-start.3 = (f32[8,3072]{1,0:T(8,128)S(1)}, f32[8,3072]{1,0:T(8,128)S(1)}, u32[]{:S(2)}, u32[]{:S(2)}) collective-permute-start(f32[8,3072]{1,0:T(8,128)S(1)} %collective-permute-done.2.refs_2_), channel_id=1, source_target_pairs={{0,4},{4,0},{8,12},{12,8},{16,20},{20,16},{24,28},{28,24},{1,5},{5... | collective-permute-start | bytes 294920 | tf_op jit(solution)/shard_map/ppermute | solution.py:17
  11.3 7.4 %collective-permute-start.1 = (f32[8,3072]{1,0:T(8,128)S(1)}, f32[8,3072]{1,0:T(8,128)S(1)}, u32[]{:S(2)}, u32[]{:S(2)}) collective-permute-start(f32[8,3072]{1,0:T(8,128)S(1)} %collective-permute-done.refs_0_), channel_id=1, source_target_pairs={{0,4},{4,0},{8,12},{12,8},{16,20},{20,16},{24,28},{28,24},{1,5},{5... | collective-permute-start | bytes 294920 | tf_op jit(solution)/shard_map/ppermute | solution.py:17
  11.3 10.4 %collective-permute-start.7 = (f32[8,3072]{1,0:T(8,128)}, f32[8,3072]{1,0:T(8,128)S(1)}, u32[]{:S(2)}, u32[]{:S(2)}) collective-permute-start(f32[8,3072]{1,0:T(8,128)} %refs_4_.1), channel_id=1, source_target_pairs={{0,24},{4,28},{8,16},{12,20},{16,8},{20,12},{24,0},{28,4},{1,25},{... | collective-permute-start | bytes 294920 | tf_op jit(solution)/shard_map/ppermute | solution.py:17
  20.1 4.9 %collective-permute-start.5 = (f32[48,640]{1,0:T(8,128)S(1)}, f32[48,640]{1,0:T(8,128)S(1)}, u32[]{:S(2)}, u32[]{:S(2)}) collective-permute-start(f32[48,640]{1,0:T(8,128)S(1)} %get-tuple-element.22), channel_id=1, source_target_pairs={{0,1},{1,0},{2,3},{3,2},{4,6},{5,7},{6,4},{7,5},{8,9},{9,8},{10,11... | collective-permute-start | bytes 368648 | tf_op jit(solution)/shard_map/ppermute | solution.py:206
  21.7 5.0 %collective-permute-start.8 = (f32[8,3072]{1,0:T(8,128)S(1)}, f32[8,3072]{1,0:T(8,128)S(1)}, u32[]{:S(2)}, u32[]{:S(2)}) collective-permute-start(f32[8,3072]{1,0:T(8,128)S(1)} %collective-permute-done.7.refs_0_), channel_id=1, source_target_pairs={{0,4},{4,0},{8,12},{12,8},{16,20},{20,16},{24,28},{28,24},{1,5},{5... | collective-permute-start | bytes 294920 | tf_op jit(solution)/shard_map/ppermute | solution.py:17
  25.1 10.9 %copy-start = (f32[64,640]{1,0:T(8,128)S(1)}, f32[64,640]{1,0:T(8,128)}, u32[]{:S(2)}) copy-start(f32[64,640]{1,0:T(8,128)} %denom.3) | copy-start | bytes 491524
  25.1 12.1 %collective-permute-start.6 = (f32[48,640]{1,0:T(8,128)S(1)}, f32[48,640]{1,0:T(8,128)S(1)}, u32[]{:S(2)}, u32[]{:S(2)}) collective-permute-start(f32[48,640]{1,0:T(8,128)S(1)} %add.27.mine), channel_id=1, source_target_pairs={{0,2},{1,3},{2,0},{3,1},{4,5},{5,4},{6,7},{7,6},{8,10},{9,11},{10,... | collective-permute-start | bytes 368648 | tf_op jit(solution)/shard_map/ppermute | solution.py:206
  27.8 4.1 %collective-permute-start.9 = (f32[16,640]{1,0:T(8,128)S(1)}, f32[16,640]{1,0:T(8,128)S(1)}, u32[]{:S(2)}, u32[]{:S(2)}) collective-permute-start(f32[16,640]{1,0:T(8,128)S(1)} %get-tuple-element.26), channel_id=1, source_target_pairs={{0,1},{1,0},{2,3},{3,2},{4,6},{5,7},{6,4},{7,5},{8,9},{9,8},{10,11... | collective-permute-start | bytes 122888 | tf_op jit(solution)/shard_map/ppermute | solution.py:206
  31.9 4.0 %collective-permute-start.10 = (f32[16,640]{1,0:T(8,128)S(1)}, f32[16,640]{1,0:T(8,128)S(1)}, u32[]{:S(2)}, u32[]{:S(2)}) collective-permute-start(f32[16,640]{1,0:T(8,128)S(1)} %add.28.mine), channel_id=1, source_target_pairs={{0,2},{1,3},{2,0},{3,1},{4,5},{5,4},{6,7},{7,6},{8,10},{9,11},{10,... | collective-permute-start | bytes 122888 | tf_op jit(solution)/shard_map/ppermute | solution.py:206
  37.1 2.1 %collective-permute-start.16 = (f32[8,3072]{1,0:T(8,128)S(1)}, f32[8,3072]{1,0:T(8,128)S(1)}, u32[]{:S(2)}, u32[]{:S(2)}) collective-permute-start(f32[8,3072]{1,0:T(8,128)S(1)} %get-tuple-element.37), channel_id=1, source_target_pairs={{0,4},{4,0},{8,12},{12,8},{16,20},{20,16},{24,28},{28,24},{1,5},{5... | collective-permute-start | bytes 294920 | tf_op jit(solution)/shard_map/ppermute | solution.py:17
  38.6 2.3 %collective-permute-start.11 = (f32[8,3072]{1,0:T(8,128)S(1)}, f32[8,3072]{1,0:T(8,128)S(1)}, u32[]{:S(2)}, u32[]{:S(2)}) collective-permute-start(f32[8,3072]{1,0:T(8,128)S(1)} %get-tuple-element.31), channel_id=1, source_target_pairs={{0,4},{4,0},{8,12},{12,8},{16,20},{20,16},{24,28},{28,24},{1,5},{5... | collective-permute-start | bytes 294920 | tf_op jit(solution)/shard_map/ppermute | solution.py:17
  39.1 1.8 %collective-permute-start.13 = (f32[8,3072]{1,0:T(8,128)S(1)}, f32[8,3072]{1,0:T(8,128)S(1)}, u32[]{:S(2)}, u32[]{:S(2)}) collective-permute-start(f32[8,3072]{1,0:T(8,128)S(1)} %get-tuple-element.33), channel_id=1, source_target_pairs={{0,4},{4,0},{8,12},{12,8},{16,20},{20,16},{24,28},{28,24},{1,5},{5... | collective-permute-start | bytes 294920 | tf_op jit(solution)/shard_map/ppermute | solution.py:17
  39.2 8.4 %collective-permute-start.17 = (f32[8,3072]{1,0:T(8,128)S(1)}, f32[8,3072]{1,0:T(8,128)S(1)}, u32[]{:S(2)}, u32[]{:S(2)}) collective-permute-start(f32[8,3072]{1,0:T(8,128)S(1)} %add.34), channel_id=1, source_target_pairs={{0,24},{4,28},{8,16},{12,20},{16,8},{20,12},{24,0},{28,4},{1,25},{... | collective-permute-start | bytes 294920 | tf_op jit(solution)/shard_map/ppermute | solution.py:17
  40.7 7.0 %collective-permute-start.15 = (f32[8,3072]{1,0:T(8,128)S(1)}, f32[8,3072]{1,0:T(8,128)S(1)}, u32[]{:S(2)}, u32[]{:S(2)}) collective-permute-start(f32[8,3072]{1,0:T(8,128)S(1)} %get-tuple-element.35), channel_id=1, source_target_pairs={{0,4},{4,0},{8,12},{12,8},{16,20},{20,16},{24,28},{28,24},{1,5},{5... | collective-permute-start | bytes 294920 | tf_op jit(solution)/shard_map/ppermute | solution.py:17
  40.9 9.6 %collective-permute-start.12 = (f32[8,3072]{1,0:T(8,128)S(1)}, f32[8,3072]{1,0:T(8,128)S(1)}, u32[]{:S(2)}, u32[]{:S(2)}) collective-permute-start(f32[8,3072]{1,0:T(8,128)S(1)} %add.29), channel_id=1, source_target_pairs={{0,16},{4,20},{8,24},{12,28},{16,0},{20,4},{24,8},{28,12},{1,17},{... | collective-permute-start | bytes 294920 | tf_op jit(solution)/shard_map/ppermute | solution.py:17
  41.0 9.4 %collective-permute-start.14 = (f32[8,3072]{1,0:T(8,128)S(1)}, f32[8,3072]{1,0:T(8,128)S(1)}, u32[]{:S(2)}, u32[]{:S(2)}) collective-permute-start(f32[8,3072]{1,0:T(8,128)S(1)} %add.30), channel_id=1, source_target_pairs={{0,8},{4,12},{8,0},{12,4},{16,24},{20,28},{24,16},{28,20},{1,9},{5... | collective-permute-start | bytes 294920 | tf_op jit(solution)/shard_map/ppermute | solution.py:17

commit v4 on v3

--- a/solution.py
+++ b/solution.py
@@ -48,9 +48,8 @@
             copy(p).wait()
             rows = pl.ds(p * piece, piece)
 
-            @pl.loop(0, width // step)
-            def _(c, rows=rows):
-                columns = pl.ds(pl.multiple_of(c * step, step), step)
+            for c in range(width // step):
+                columns = pl.ds(c * step, step)
                 a, b = split(held[rows, columns])
                 hi[rows, columns], lo[rows, columns] = a, b
                 hi_t[columns, rows], lo_t[columns, rows] = a.T, b.T
@@ -186,7 +185,7 @@
 
 def chunks_of(rows):
     chips = range(1, rows // 2)
-    last = [k for k in chips if k % 4 == 3]
+    last = [k for k in chips if k % 2 and k > 1]
     return [[*sorted(set(chips) - set(last), reverse=True), 0], last]
 
 
@@ -213,7 +212,10 @@
 
     blocks = {0: factor_ia}
     for k in range(1, rows // 2):
-        blocks[2 * k] = swap(factor_ia, "row", 2 * k)
+        if k % 2 and k > 1:
+            blocks[2 * k] = swap(blocks[2 * k - 2], "row", 2)
+        else:
+            blocks[2 * k] = swap(factor_ia, "row", 2 * k)
     for d in range(0, rows, 2):
         blocks[d + 1] = swap(blocks[d], "row", 1)
     jb_hi, jb_lo, hi_t, lo_t = prepare(factor_jb)

time: 51.3 us -> 50 us (0.975)
  starting transfers between devices: 18.8 us -> 17 us
  waiting for transfers between devices: 17 us -> 18.2 us
  Pallas kernels: 13.8 us -> 13.1 us
    ppermute x14, starting transfers between devices: 13.6 us -> 11.8 us  [swap(): return lax.ppermute(x, axis, [(i, i ^ distance) for i in range(size)])]
    ppermute x14, waiting for transfers between devices: 7.6 us -> 8.82 us  [swap(): return lax.ppermute(x, axis, [(i, i ^ distance) for i in range(size)])]
    pallas_call x1, Pallas kernels: 4.91 us -> 4.25 us  [prepare(): pl.pallas_call(kernel, name='prepare', out_shape=(plain, plain, turned, t...]
  transfers between devices with their start and end apart: 18 -> 18, of which waited for: 6 -> 6; matrix products, arithmetic and copies ran while one was open for 0% -> 0% of each run, Pallas kernels for 27% -> 26%
where the time goes in v4:
time: 50 us; the launch traced here: 49.9 us
  waiting for transfers between devices  18.2 us (36%)
  starting transfers between devices  17 us (34%)
  Pallas kernels  13.1 us (26%)
  between operations  0.76 us (2%)
  other arithmetic  0.74 us (1%)
    ppermute x14, starting transfers between devices, swap(): return lax.ppermute(x, axis, [(i, i ^ distance) for i in range(size)])  11.8 us
    ppermute x4, waiting for transfers between devices, exchange(): return lax.ppermute(x, ('row', 'aux'), pairs)  9.38 us
    ppermute x14, waiting for transfers between devices, swap(): return lax.ppermute(x, axis, [(i, i ^ distance) for i in range(size)])  8.82 us
    ppermute x4, starting transfers between devices, exchange(): return lax.ppermute(x, ('row', 'aux'), pairs)  5.21 us
    pallas_call x1, Pallas kernels, prepare(): pl.pallas_call(kernel, name='prepare', out_shape=(plain, plain, turned, t...  4.25 us
    pallas_call x1, Pallas kernels, gradient_jb(): pl.pallas_call(kernel, name='gradient_jb', out_shape=jax.ShapeDtypeStruct...  3.66 us
    pallas_call x2, Pallas kernels, gradient_share(): pl.pallas_call(kernel, out_shape=(jax.ShapeDtypeStruct((2 * rows, columns...  2.61 us
    pallas_call x2, Pallas kernels, integral_share(): pl.pallas_call(kernel, out_shape=(jax.ShapeDtypeStruct((rows, columns), F...  2.61 us
  transfers between devices with their start and end apart: 18, of which 6 were waited for; matrix products, arithmetic and copies ran while one was open for 0% of the time, Pallas kernels for 26%

profile of v4, /device:TPU:0, one launch (start us, length us, event | category | flops | bytes accessed | tf_op | source)
XLA Modules:
  0.0 49.9 jit_solution(15963312250512074499)
XLA Ops:
  0.6 0.0 copy-start.1
  0.6 3.1 %collective-permute-start.2 = (f32[8,3072]{1,0:T(8,128)}, f32[8,3072]{1,0:T(8,128)S(1)}, u32[]{:S(2)}, u32[]{:S(2)}) collective-permute-start(f32[8,3072]{1,0:T(8,128)} %refs_4_.1), channel_id=1, source_target_pairs={{0,8},{4,12},{8,0},{12,4},{16,24},{20,28},{24,16},{28,20},{1,9},{5... | collective-permute-start | bytes 294920 | tf_op jit(solution)/shard_map/ppermute | solution.py:17
  3.8 2.6 %collective-permute-start = (f32[8,3072]{1,0:T(8,128)}, f32[8,3072]{1,0:T(8,128)S(1)}, u32[]{:S(2)}, u32[]{:S(2)}) collective-permute-start(f32[8,3072]{1,0:T(8,128)} %refs_4_.1), channel_id=1, source_target_pairs={{0,16},{4,20},{8,24},{12,28},{16,0},{20,4},{24,8},{28,12},{1,17},{... | collective-permute-start | bytes 294920 | tf_op jit(solution)/shard_map/ppermute | solution.py:17
  6.3 0.0 collective-permute-start.4
  6.3 0.4 collective-permute-done.2.refs_2_
  6.8 0.1 collective-permute-start.3
  6.9 4.4 %collective-permute-done.refs_0_ = f32[8,3072]{1,0:T(8,128)S(1)} collective-permute-done((f32[8,3072]{1,0:T(8,128)}, f32[8,3072]{1,0:T(8,128)S(1)}, u32[]{:S(2)}, u32[]{:S(2)}) %collective-permute-start) | collective-permute-done | bytes 98336 | tf_op jit(solution)/shard_map/ppermute | solution.py:17
  11.3 0.0 collective-permute-start.1
  11.3 0.3 collective-permute-start.7
  11.6 4.3 %prepare.1 = (bf16[640,3072]{1,0:T(8,128)(2,1)S(1)}, bf16[640,3072]{1,0:T(8,128)(2,1)S(1)}, bf16[3072,640]{1,0:T(8,128)(2,1)S(1)}, bf16[3072,640]{1,0:T(8,128)(2,1)S(1)}) custom-call(f32[640,3072]{1,0:T(8,128)} %jb.1), custom_call_target="tpu_custom_call" | custom-call | flops 7864320 | bytes 7864320 | tf_op jit(solution)/shard_map/prepare/pallas_call | solution.py:59
  15.9 0.0 collective-permute-done.4.refs_5_
  15.9 0.0 collective-permute-done.3.refs_3_
  15.9 0.0 collective-permute-done.1.refs_1_
  15.9 0.0 copy-done.1
  15.9 1.4 %shard_map.50 = (f32[48,640]{1,0:T(8,128)S(1)}, bf16[96,3072]{1,0:T(8,128)(2,1)S(1)}) custom-call(f32[8,3072]{1,0:T(8,128)S(1)} %collective-permute-done.refs_0_, f32[8,3072]{1,0:T(8,128)S(1)} %collective-permute-done.1.refs_1_, f32[8,3072]{1,0:T(8,128)S(1)} %collective-permute-done.2.refs_2_, f32[8,3072]{1,0:T(8,128)S(1)} %collective-permute-done.3.refs_3_, ...), custom_call_target="tpu_custom_call" | custom-call | flops 566231040 | bytes 1048576 | tf_op jit(solution)/shard_map/pallas_call | solution.py:92
  17.4 1.6 %collective-permute-start.5 = (f32[48,640]{1,0:T(8,128)S(1)}, f32[48,640]{1,0:T(8,128)S(1)}, u32[]{:S(2)}, u32[]{:S(2)}) collective-permute-start(f32[48,640]{1,0:T(8,128)S(1)} %get-tuple-element.22), channel_id=1, source_target_pairs={{0,1},{1,0},{2,3},{3,2},{4,6},{5,7},{6,4},{7,5},{8,9},{9,8},{10,11... | collective-permute-start | bytes 368648 | tf_op jit(solution)/shard_map/ppermute | solution.py:205
  18.9 0.0 collective-permute-done.7.refs_0_
  18.9 0.0 collective-permute-start.8
  18.9 3.4 %collective-permute-done.5 = f32[48,640]{1,0:T(8,128)S(1)} collective-permute-done((f32[48,640]{1,0:T(8,128)S(1)}, f32[48,640]{1,0:T(8,128)S(1)}, u32[]{:S(2)}, u32[]{:S(2)}) %collective-permute-start.5) | collective-permute-done | bytes 122912 | tf_op jit(solution)/shard_map/ppermute | solution.py:205
  22.3 0.0 copy-start
  22.4 1.6 %collective-permute-start.6 = (f32[48,640]{1,0:T(8,128)S(1)}, f32[48,640]{1,0:T(8,128)S(1)}, u32[]{:S(2)}, u32[]{:S(2)}) collective-permute-start(f32[48,640]{1,0:T(8,128)S(1)} %add.27.mine), channel_id=1, source_target_pairs={{0,2},{1,3},{2,0},{3,1},{4,5},{5,4},{6,7},{7,6},{8,10},{9,11},{10,... | collective-permute-start | bytes 368648 | tf_op jit(solution)/shard_map/ppermute | solution.py:205
  23.9 0.0 collective-permute-done.8.refs_1_
  23.9 1.2 %shard_map.52 = (f32[16,640]{1,0:T(8,128)S(1)}, bf16[32,3072]{1,0:T(8,128)(2,1)S(1)}) custom-call(f32[8,3072]{1,0:T(8,128)S(1)} %collective-permute-done.7.refs_0_, f32[8,3072]{1,0:T(8,128)S(1)} %collective-permute-done.8.refs_1_, bf16[3072,640]{1,0:T(8,128)(2,1)S(1)} %get-tuple-element.20.refs_6_.refs_2_, ...), custom_call_target="tpu_custom_call" | custom-call | flops 188743680 | bytes 1048576 | tf_op jit(solution)/shard_map/pallas_call | solution.py:92
  25.1 1.6 %collective-permute-start.9 = (f32[16,640]{1,0:T(8,128)S(1)}, f32[16,640]{1,0:T(8,128)S(1)}, u32[]{:S(2)}, u32[]{:S(2)}) collective-permute-start(f32[16,640]{1,0:T(8,128)S(1)} %get-tuple-element.26), channel_id=1, source_target_pairs={{0,1},{1,0},{2,3},{3,2},{4,6},{5,7},{6,4},{7,5},{8,9},{9,8},{10,11... | collective-permute-start | bytes 122888 | tf_op jit(solution)/shard_map/ppermute | solution.py:205
  26.7 2.5 %collective-permute-done.9 = f32[16,640]{1,0:T(8,128)S(1)} collective-permute-done((f32[16,640]{1,0:T(8,128)S(1)}, f32[16,640]{1,0:T(8,128)S(1)}, u32[]{:S(2)}, u32[]{:S(2)}) %collective-permute-start.9) | collective-permute-done | bytes 40992 | tf_op jit(solution)/shard_map/ppermute | solution.py:205
  29.2 0.5 %collective-permute-start.10 = (f32[16,640]{1,0:T(8,128)S(1)}, f32[16,640]{1,0:T(8,128)S(1)}, u32[]{:S(2)}, u32[]{:S(2)}) collective-permute-start(f32[16,640]{1,0:T(8,128)S(1)} %add.28.mine), channel_id=1, source_target_pairs={{0,2},{1,3},{2,0},{3,1},{4,5},{5,4},{6,7},{7,6},{8,10},{9,11},{10,... | collective-permute-start | bytes 122888 | tf_op jit(solution)/shard_map/ppermute | solution.py:205
  29.7 3.5 %collective-permute-done.10.theirs = f32[16,640]{1,0:T(8,128)S(1)} collective-permute-done((f32[16,640]{1,0:T(8,128)S(1)}, f32[16,640]{1,0:T(8,128)S(1)}, u32[]{:S(2)}, u32[]{:S(2)}) %collective-permute-start.10) | collective-permute-done | bytes 40992 | tf_op jit(solution)/shard_map/ppermute | solution.py:205
  33.2 0.0 copy-done
  33.2 1.2 %shard_map.53 = (bf16[32,640]{1,0:T(8,128)(2,1)S(1)}, f32[8,3072]{1,0:T(8,128)S(1)}, f32[8,3072]{1,0:T(8,128)S(1)}) custom-call(f32[16,640]{1,0:T(8,128)S(1)} %add.28.mine, f32[16,640]{1,0:T(8,128)S(1)} %collective-permute-done.10.theirs, f32[64,640]{1,0:T(8,128)S(1)} %copy-done, bf16[640,3072]{1,0:T(8,128)(2,1)S(1)} %get-tuple-element.23.hi, ...), custom_call_target="tpu_custom_call" | custom-call | flops 188743680 | bytes 1048576 | tf_op jit(solution)/shard_map/pallas_call | solution.py:127
  34.4 0.0 collective-permute-start.16
  34.4 0.0 collective-permute-done.6.theirs
  34.4 1.4 %shard_map.51 = (bf16[96,640]{1,0:T(8,128)(2,1)S(1)}, f32[8,3072]{1,0:T(8,128)S(1)}, f32[8,3072]{1,0:T(8,128)S(1)}, f32[8,3072]{1,0:T(8,128)S(1)}, f32[8,3072]{1...) custom-call(f32[48,640]{1,0:T(8,128)S(1)} %add.27.mine, f32[48,640]{1,0:T(8,128)S(1)} %collective-permute-done.6.theirs, ...), custom_call_target="tpu_custom_call" | custom-call | flops 566231040 | bytes 1048576 | tf_op jit(solution)/shard_map/pallas_call | solution.py:127
  35.8 0.6 %collective-permute-start.11 = (f32[8,3072]{1,0:T(8,128)S(1)}, f32[8,3072]{1,0:T(8,128)S(1)}, u32[]{:S(2)}, u32[]{:S(2)}) collective-permute-start(f32[8,3072]{1,0:T(8,128)S(1)} %get-tuple-element.31), channel_id=1, source_target_pairs={{0,4},{4,0},{8,12},{12,8},{16,20},{20,16},{24,28},{28,24},{1,5},{5... | collective-permute-start | bytes 294920 | tf_op jit(solution)/shard_map/ppermute | solution.py:17
  36.4 0.1 collective-permute-start.13
  36.5 0.4 collective-permute-start.15
  36.9 0.0 collective-permute-done.16
  36.9 2.1 %collective-permute-start.17 = (f32[8,3072]{1,0:T(8,128)S(1)}, f32[8,3072]{1,0:T(8,128)S(1)}, u32[]{:S(2)}, u32[]{:S(2)}) collective-permute-start(f32[8,3072]{1,0:T(8,128)S(1)} %add.34), channel_id=1, source_target_pairs={{0,24},{4,28},{8,16},{12,20},{16,8},{20,12},{24,0},{28,4},{1,25},{... | collective-permute-start | bytes 294920 | tf_op jit(solution)/shard_map/ppermute | solution.py:17
  39.1 0.0 collective-permute-done.11
  39.1 1.1 %collective-permute-start.12 = (f32[8,3072]{1,0:T(8,128)S(1)}, f32[8,3072]{1,0:T(8,128)S(1)}, u32[]{:S(2)}, u32[]{:S(2)}) collective-permute-start(f32[8,3072]{1,0:T(8,128)S(1)} %add.29), channel_id=1, source_target_pairs={{0,16},{4,20},{8,24},{12,28},{16,0},{20,4},{24,8},{28,12},{1,17},{... | collective-permute-start | bytes 294920 | tf_op jit(solution)/shard_map/ppermute | solution.py:17
  40.2 0.0 collective-permute-done.13
  40.2 1.3 %collective-permute-start.14 = (f32[8,3072]{1,0:T(8,128)S(1)}, f32[8,3072]{1,0:T(8,128)S(1)}, u32[]{:S(2)}, u32[]{:S(2)}) collective-permute-start(f32[8,3072]{1,0:T(8,128)S(1)} %add.30), channel_id=1, source_target_pairs={{0,8},{4,12},{8,0},{12,4},{16,24},{20,28},{24,16},{28,20},{1,9},{5... | collective-permute-start | bytes 294920 | tf_op jit(solution)/shard_map/ppermute | solution.py:17
  41.6 3.7 %gradient_jb.1 = f32[640,3072]{1,0:T(8,128)} custom-call(bf16[96,640]{1,0:T(8,128)(2,1)S(1)} %get-tuple-element.25.refs_0_, bf16[32,640]{1,0:T(8,128)(2,1)S(1)} %get-tuple-element.27.refs_1_, bf16[96,3072]{1,0:T(8,128)(2,1)S(1)} %get-tuple-element.28.refs_2_, bf16[32,3072]{1,0:T(8,128)(2,1)S(1)} %get-tuple-element.29.refs_3_), custom_call_target="tpu_custom_call" | custom-call | flops 754974720 | bytes 7864320 | tf_op jit(solution)/shard_map/gradient_jb/pallas_call | solution.py:168
  45.2 0.0 collective-permute-done.15
  45.2 0.0 collective-permute-done.17
  45.3 4.0 %collective-permute-done.12 = f32[8,3072]{1,0:T(8,128)S(1)} collective-permute-done((f32[8,3072]{1,0:T(8,128)S(1)}, f32[8,3072]{1,0:T(8,128)S(1)}, u32[]{:S(2)}, u32[]{:S(2)}) %collective-permute-start.12) | collective-permute-done | bytes 98336 | tf_op jit(solution)/shard_map/ppermute | solution.py:17
  49.2 0.0 collective-permute-done.14
  49.2 0.7 %add_add_fusion = f32[8,3072]{1,0:T(8,128)} fusion(f32[8,3072]{1,0:T(8,128)S(1)} %collective-permute-done.17, f32[8,3072]{1,0:T(8,128)S(1)} %get-tuple-element.34, f32[8,3072]{1,0:T(8,128)S(1)} %collective-permute-done.15, f32[8,3072]{1,0:T(8,128)S(1)} %collective-permute-done.12, f32[8,3072]{1,0:T(8,128)S(1)} %collective-permute-done.14), kind=kLoop, calls=%fused_computation | loop fusion | flops 98304 | bytes 589824 | tf_op jit(solution)/shard_map/add | solution.py:239
  (5 shorter events, 0.1 us)
Async XLA Ops:
  0.6 15.3 %copy-start.1 = (f32[8,3072]{1,0:T(8,128)S(1)}, f32[8,3072]{1,0:T(8,128)}, u32[]{:S(2)}) copy-start(f32[8,3072]{1,0:T(8,128)} %refs_4_.1) | copy-start | bytes 294916
  0.6 6.1 %collective-permute-start.2 = (f32[8,3072]{1,0:T(8,128)}, f32[8,3072]{1,0:T(8,128)S(1)}, u32[]{:S(2)}, u32[]{:S(2)}) collective-permute-start(f32[8,3072]{1,0:T(8,128)} %refs_4_.1), channel_id=1, source_target_pairs={{0,8},{4,12},{8,0},{12,4},{16,24},{20,28},{24,16},{28,20},{1,9},{5... | collective-permute-start | bytes 294920 | tf_op jit(solution)/shard_map/ppermute | solution.py:17
  3.8 7.5 %collective-permute-start = (f32[8,3072]{1,0:T(8,128)}, f32[8,3072]{1,0:T(8,128)S(1)}, u32[]{:S(2)}, u32[]{:S(2)}) collective-permute-start(f32[8,3072]{1,0:T(8,128)} %refs_4_.1), channel_id=1, source_target_pairs={{0,16},{4,20},{8,24},{12,28},{16,0},{20,4},{24,8},{28,12},{1,17},{... | collective-permute-start | bytes 294920 | tf_op jit(solution)/shard_map/ppermute | solution.py:17
  6.3 9.5 %collective-permute-start.4 = (f32[8,3072]{1,0:T(8,128)}, f32[8,3072]{1,0:T(8,128)S(1)}, u32[]{:S(2)}, u32[]{:S(2)}) collective-permute-start(f32[8,3072]{1,0:T(8,128)} %refs_4_.1), channel_id=1, source_target_pairs={{0,4},{4,0},{8,12},{12,8},{16,20},{20,16},{24,28},{28,24},{1,5},{5... | collective-permute-start | bytes 294920 | tf_op jit(solution)/shard_map/ppermute | solution.py:17
  6.8 9.1 %collective-permute-start.3 = (f32[8,3072]{1,0:T(8,128)S(1)}, f32[8,3072]{1,0:T(8,128)S(1)}, u32[]{:S(2)}, u32[]{:S(2)}) collective-permute-start(f32[8,3072]{1,0:T(8,128)S(1)} %collective-permute-done.2.refs_2_), channel_id=1, source_target_pairs={{0,4},{4,0},{8,12},{12,8},{16,20},{20,16},{24,28},{28,24},{1,5},{5... | collective-permute-start | bytes 294920 | tf_op jit(solution)/shard_map/ppermute | solution.py:17
  11.3 4.6 %collective-permute-start.1 = (f32[8,3072]{1,0:T(8,128)S(1)}, f32[8,3072]{1,0:T(8,128)S(1)}, u32[]{:S(2)}, u32[]{:S(2)}) collective-permute-start(f32[8,3072]{1,0:T(8,128)S(1)} %collective-permute-done.refs_0_), channel_id=1, source_target_pairs={{0,4},{4,0},{8,12},{12,8},{16,20},{20,16},{24,28},{28,24},{1,5},{5... | collective-permute-start | bytes 294920 | tf_op jit(solution)/shard_map/ppermute | solution.py:17
  11.3 7.6 %collective-permute-start.7 = (f32[8,3072]{1,0:T(8,128)S(1)}, f32[8,3072]{1,0:T(8,128)S(1)}, u32[]{:S(2)}, u32[]{:S(2)}) collective-permute-start(f32[8,3072]{1,0:T(8,128)S(1)} %collective-permute-done.refs_0_), channel_id=1, source_target_pairs={{0,8},{4,12},{8,0},{12,4},{16,24},{20,28},{24,16},{28,20},{1,9},{5... | collective-permute-start | bytes 294920 | tf_op jit(solution)/shard_map/ppermute | solution.py:17
  17.4 4.9 %collective-permute-start.5 = (f32[48,640]{1,0:T(8,128)S(1)}, f32[48,640]{1,0:T(8,128)S(1)}, u32[]{:S(2)}, u32[]{:S(2)}) collective-permute-start(f32[48,640]{1,0:T(8,128)S(1)} %get-tuple-element.22), channel_id=1, source_target_pairs={{0,1},{1,0},{2,3},{3,2},{4,6},{5,7},{6,4},{7,5},{8,9},{9,8},{10,11... | collective-permute-start | bytes 368648 | tf_op jit(solution)/shard_map/ppermute | solution.py:205
  18.9 5.0 %collective-permute-start.8 = (f32[8,3072]{1,0:T(8,128)S(1)}, f32[8,3072]{1,0:T(8,128)S(1)}, u32[]{:S(2)}, u32[]{:S(2)}) collective-permute-start(f32[8,3072]{1,0:T(8,128)S(1)} %collective-permute-done.7.refs_0_), channel_id=1, source_target_pairs={{0,4},{4,0},{8,12},{12,8},{16,20},{20,16},{24,28},{28,24},{1,5},{5... | collective-permute-start | bytes 294920 | tf_op jit(solution)/shard_map/ppermute | solution.py:17
  22.3 10.9 %copy-start = (f32[64,640]{1,0:T(8,128)S(1)}, f32[64,640]{1,0:T(8,128)}, u32[]{:S(2)}) copy-start(f32[64,640]{1,0:T(8,128)} %denom.3) | copy-start | bytes 491524
  22.4 12.1 %collective-permute-start.6 = (f32[48,640]{1,0:T(8,128)S(1)}, f32[48,640]{1,0:T(8,128)S(1)}, u32[]{:S(2)}, u32[]{:S(2)}) collective-permute-start(f32[48,640]{1,0:T(8,128)S(1)} %add.27.mine), channel_id=1, source_target_pairs={{0,2},{1,3},{2,0},{3,1},{4,5},{5,4},{6,7},{7,6},{8,10},{9,11},{10,... | collective-permute-start | bytes 368648 | tf_op jit(solution)/shard_map/ppermute | solution.py:205
  25.1 4.1 %collective-permute-start.9 = (f32[16,640]{1,0:T(8,128)S(1)}, f32[16,640]{1,0:T(8,128)S(1)}, u32[]{:S(2)}, u32[]{:S(2)}) collective-permute-start(f32[16,640]{1,0:T(8,128)S(1)} %get-tuple-element.26), channel_id=1, source_target_pairs={{0,1},{1,0},{2,3},{3,2},{4,6},{5,7},{6,4},{7,5},{8,9},{9,8},{10,11... | collective-permute-start | bytes 122888 | tf_op jit(solution)/shard_map/ppermute | solution.py:205
  29.2 4.0 %collective-permute-start.10 = (f32[16,640]{1,0:T(8,128)S(1)}, f32[16,640]{1,0:T(8,128)S(1)}, u32[]{:S(2)}, u32[]{:S(2)}) collective-permute-start(f32[16,640]{1,0:T(8,128)S(1)} %add.28.mine), channel_id=1, source_target_pairs={{0,2},{1,3},{2,0},{3,1},{4,5},{5,4},{6,7},{7,6},{8,10},{9,11},{10,... | collective-permute-start | bytes 122888 | tf_op jit(solution)/shard_map/ppermute | solution.py:205
  34.4 2.5 %collective-permute-start.16 = (f32[8,3072]{1,0:T(8,128)S(1)}, f32[8,3072]{1,0:T(8,128)S(1)}, u32[]{:S(2)}, u32[]{:S(2)}) collective-permute-start(f32[8,3072]{1,0:T(8,128)S(1)} %get-tuple-element.37), channel_id=1, source_target_pairs={{0,4},{4,0},{8,12},{12,8},{16,20},{20,16},{24,28},{28,24},{1,5},{5... | collective-permute-start | bytes 294920 | tf_op jit(solution)/shard_map/ppermute | solution.py:17
  35.8 3.3 %collective-permute-start.11 = (f32[8,3072]{1,0:T(8,128)S(1)}, f32[8,3072]{1,0:T(8,128)S(1)}, u32[]{:S(2)}, u32[]{:S(2)}) collective-permute-start(f32[8,3072]{1,0:T(8,128)S(1)} %get-tuple-element.31), channel_id=1, source_target_pairs={{0,4},{4,0},{8,12},{12,8},{16,20},{20,16},{24,28},{28,24},{1,5},{5... | collective-permute-start | bytes 294920 | tf_op jit(solution)/shard_map/ppermute | solution.py:17
  36.4 3.8 %collective-permute-start.13 = (f32[8,3072]{1,0:T(8,128)S(1)}, f32[8,3072]{1,0:T(8,128)S(1)}, u32[]{:S(2)}, u32[]{:S(2)}) collective-permute-start(f32[8,3072]{1,0:T(8,128)S(1)} %get-tuple-element.33), channel_id=1, source_target_pairs={{0,4},{4,0},{8,12},{12,8},{16,20},{20,16},{24,28},{28,24},{1,5},{5... | collective-permute-start | bytes 294920 | tf_op jit(solution)/shard_map/ppermute | solution.py:17
  36.5 8.7 %collective-permute-start.15 = (f32[8,3072]{1,0:T(8,128)S(1)}, f32[8,3072]{1,0:T(8,128)S(1)}, u32[]{:S(2)}, u32[]{:S(2)}) collective-permute-start(f32[8,3072]{1,0:T(8,128)S(1)} %get-tuple-element.35), channel_id=1, source_target_pairs={{0,4},{4,0},{8,12},{12,8},{16,20},{20,16},{24,28},{28,24},{1,5},{5... | collective-permute-start | bytes 294920 | tf_op jit(solution)/shard_map/ppermute | solution.py:17
  36.9 8.3 %collective-permute-start.17 = (f32[8,3072]{1,0:T(8,128)S(1)}, f32[8,3072]{1,0:T(8,128)S(1)}, u32[]{:S(2)}, u32[]{:S(2)}) collective-permute-start(f32[8,3072]{1,0:T(8,128)S(1)} %add.34), channel_id=1, source_target_pairs={{0,24},{4,28},{8,16},{12,20},{16,8},{20,12},{24,0},{28,4},{1,25},{... | collective-permute-start | bytes 294920 | tf_op jit(solution)/shard_map/ppermute | solution.py:17
  39.1 10.1 %collective-permute-start.12 = (f32[8,3072]{1,0:T(8,128)S(1)}, f32[8,3072]{1,0:T(8,128)S(1)}, u32[]{:S(2)}, u32[]{:S(2)}) collective-permute-start(f32[8,3072]{1,0:T(8,128)S(1)} %add.29), channel_id=1, source_target_pairs={{0,16},{4,20},{8,24},{12,28},{16,0},{20,4},{24,8},{28,12},{1,17},{... | collective-permute-start | bytes 294920 | tf_op jit(solution)/shard_map/ppermute | solution.py:17
  40.2 9.0 %collective-permute-start.14 = (f32[8,3072]{1,0:T(8,128)S(1)}, f32[8,3072]{1,0:T(8,128)S(1)}, u32[]{:S(2)}, u32[]{:S(2)}) collective-permute-start(f32[8,3072]{1,0:T(8,128)S(1)} %add.30), channel_id=1, source_target_pairs={{0,8},{4,12},{8,0},{12,4},{16,24},{20,28},{24,16},{28,20},{1,9},{5... | collective-permute-start | bytes 294920 | tf_op jit(solution)/shard_map/ppermute | solution.py:17

commit v5 on v4

--- a/solution.py
+++ b/solution.py
@@ -198,6 +198,8 @@
     steps = aux_steps(aux)
 
     def partner(row, column):
+        if straight(aux):
+            return row * aux + (column ^ ((1, 2, 3), (2, 1, 3))[row % 2][step])
         bit = (step + row % 2 * (steps // 2)) % steps
         return row * aux + (column ^ 1 << bit)
 
@@ -205,9 +207,23 @@
     return lax.ppermute(x, ("row", "aux"), pairs)
 
 
+def straight(aux):
+    return aux == 4
+
+
+def aux_sum(share):
+    aux = lax.axis_size("aux")
+    steps = aux_steps(aux)
+    if straight(aux):
+        one, two, three = (exchange(share, step) for step in range(3))
+        return share + one, two + three
+    for step in range(steps - 1):
+        share = share + exchange(share, step)
+    return share, exchange(share, steps - 1)
+
+
 def per_device(factor_ia, factor_jb, denominators):
     rows = lax.axis_size("row")
-    aux = lax.axis_size("aux")
     height = factor_ia.shape[0]
 
     blocks = {0: factor_ia}
@@ -224,12 +240,11 @@
     for ks in chunks_of(rows):
         distances = [d for k in ks for d in (2 * k, 2 * k + 1)]
         share, ia = integral_share([blocks[d] for d in distances], hi_t, lo_t)
-        for step in range(aux_steps(aux) - 1):
-            share = share + exchange(share, step)
-        theirs = exchange(share, aux_steps(aux) - 1)
-        amp, outs = gradient_share(share, theirs, denominators, jb_hi, jb_lo, distances, height)
+        mine, theirs = aux_sum(share)
+        amp, outs = gradient_share(mine, theirs, denominators, jb_hi, jb_lo, distances, height)
         for k in ks:
-            folded = outs[2 * k] + swap(outs[2 * k + 1], "row", 1)
+            theirs = swap(outs[2 * k + 1], "row", 1)
+            folded = outs[2 * k] + theirs
             sums.append(swap(folded, "row", 2 * k) if k else folded)
         amp_parts.append(amp)
         ia_parts.append(ia)

time: 50 us -> 44.1 us (0.88)
  waiting for transfers between devices: 18.2 us -> 10.3 us
  starting transfers between devices: 17 us -> 18.9 us
    ppermute x4 -> x6, waiting for transfers between devices: 9.38 us -> 1.37 us  [exchange(): return lax.ppermute(x, ('row', 'aux'), pairs)]
    ppermute x4 -> x6, starting transfers between devices: 5.21 us -> 7.11 us  [exchange(): return lax.ppermute(x, ('row', 'aux'), pairs)]
  transfers between devices with their start and end apart: 18 -> 20, of which waited for: 6 -> 7; matrix products, arithmetic and copies ran while one was open for 0% -> 0% of each run, Pallas kernels for 26% -> 30%
where the time goes in v5:
time: 44.1 us; the launch traced here: 44 us
  starting transfers between devices  18.9 us (43%)
  Pallas kernels  13.2 us (30%)
  waiting for transfers between devices  10.3 us (23%)
  between operations  0.81 us (2%)
  other arithmetic  0.76 us (2%)
    ppermute x14, starting transfers between devices, swap(): return lax.ppermute(x, axis, [(i, i ^ distance) for i in range(size)])  11.8 us
    ppermute x14, waiting for transfers between devices, swap(): return lax.ppermute(x, axis, [(i, i ^ distance) for i in range(size)])  8.93 us
    ppermute x6, starting transfers between devices, exchange(): return lax.ppermute(x, ('row', 'aux'), pairs)  7.11 us
    pallas_call x1, Pallas kernels, prepare(): pl.pallas_call(kernel, name='prepare', out_shape=(plain, plain, turned, t...  4.25 us
    pallas_call x1, Pallas kernels, gradient_jb(): pl.pallas_call(kernel, name='gradient_jb', out_shape=jax.ShapeDtypeStruct...  3.66 us
    pallas_call x2, Pallas kernels, gradient_share(): pl.pallas_call(kernel, out_shape=(jax.ShapeDtypeStruct((2 * rows, columns...  2.67 us
    pallas_call x2, Pallas kernels, integral_share(): pl.pallas_call(kernel, out_shape=(jax.ShapeDtypeStruct((rows, columns), F...  2.61 us
    ppermute x6, waiting for transfers between devices, exchange(): return lax.ppermute(x, ('row', 'aux'), pairs)  1.37 us
  transfers between devices with their start and end apart: 20, of which 7 were waited for; matrix products, arithmetic and copies ran while one was open for 0% of the time, Pallas kernels for 30%

profile of v5, /device:TPU:0, one launch (start us, length us, event | category | flops | bytes accessed | tf_op | source)
XLA Modules:
  0.0 44.0 jit_solution(9794241999341734915)
XLA Ops:
  0.6 3.1 %collective-permute-start.2 = (f32[8,3072]{1,0:T(8,128)}, f32[8,3072]{1,0:T(8,128)S(1)}, u32[]{:S(2)}, u32[]{:S(2)}) collective-permute-start(f32[8,3072]{1,0:T(8,128)} %refs_4_.1), channel_id=1, source_target_pairs={{0,8},{4,12},{8,0},{12,4},{16,24},{20,28},{24,16},{28,20},{1,9},{5... | collective-permute-start | bytes 294920 | tf_op jit(solution)/shard_map/ppermute | solution.py:17
  3.8 2.6 %collective-permute-start = (f32[8,3072]{1,0:T(8,128)}, f32[8,3072]{1,0:T(8,128)S(1)}, u32[]{:S(2)}, u32[]{:S(2)}) collective-permute-start(f32[8,3072]{1,0:T(8,128)} %refs_4_.1), channel_id=1, source_target_pairs={{0,16},{4,20},{8,24},{12,28},{16,0},{20,4},{24,8},{28,12},{1,17},{... | collective-permute-start | bytes 294920 | tf_op jit(solution)/shard_map/ppermute | solution.py:17
  6.3 0.0 collective-permute-start.4
  6.3 0.4 collective-permute-done.2.refs_2_
  6.8 0.1 collective-permute-start.3
  6.9 4.4 %collective-permute-done.refs_0_ = f32[8,3072]{1,0:T(8,128)S(1)} collective-permute-done((f32[8,3072]{1,0:T(8,128)}, f32[8,3072]{1,0:T(8,128)S(1)}, u32[]{:S(2)}, u32[]{:S(2)}) %collective-permute-start) | collective-permute-done | bytes 98336 | tf_op jit(solution)/shard_map/ppermute | solution.py:17
  11.3 0.0 collective-permute-start.1
  11.3 0.3 collective-permute-start.8
  11.6 4.3 %prepare.1 = (bf16[640,3072]{1,0:T(8,128)(2,1)S(1)}, bf16[640,3072]{1,0:T(8,128)(2,1)S(1)}, bf16[3072,640]{1,0:T(8,128)(2,1)S(1)}, bf16[3072,640]{1,0:T(8,128)(2,1)S(1)}) custom-call(f32[640,3072]{1,0:T(8,128)} %jb.1), custom_call_target="tpu_custom_call" | custom-call | flops 7864320 | bytes 7864320 | tf_op jit(solution)/shard_map/prepare/pallas_call | solution.py:59
  15.9 0.0 collective-permute-done.4.refs_5_
  15.9 0.0 collective-permute-done.3.refs_3_
  15.9 0.0 collective-permute-done.1.refs_1_
  15.9 1.4 %shard_map.50 = (f32[48,640]{1,0:T(8,128)S(1)}, bf16[96,3072]{1,0:T(8,128)(2,1)S(1)}) custom-call(f32[8,3072]{1,0:T(8,128)S(1)} %collective-permute-done.refs_0_, f32[8,3072]{1,0:T(8,128)S(1)} %collective-permute-done.1.refs_1_, f32[8,3072]{1,0:T(8,128)S(1)} %collective-permute-done.2.refs_2_, f32[8,3072]{1,0:T(8,128)S(1)} %collective-permute-done.3.refs_3_, ...), custom_call_target="tpu_custom_call" | custom-call | flops 566231040 | bytes 1048576 | tf_op jit(solution)/shard_map/pallas_call | solution.py:92
  17.4 0.0 copy-start
  17.4 1.6 %collective-permute-start.5 = (f32[48,640]{1,0:T(8,128)S(1)}, f32[48,640]{1,0:T(8,128)S(1)}, u32[]{:S(2)}, u32[]{:S(2)}) collective-permute-start(f32[48,640]{1,0:T(8,128)S(1)} %get-tuple-element.22), channel_id=1, source_target_pairs={{0,1},{1,0},{2,3},{3,2},{4,6},{5,7},{6,4},{7,5},{8,9},{9,8},{10,11... | collective-permute-start | bytes 368648 | tf_op jit(solution)/shard_map/ppermute | solution.py:207
  18.9 1.5 %collective-permute-start.7 = (f32[48,640]{1,0:T(8,128)S(1)}, f32[48,640]{1,0:T(8,128)S(1)}, u32[]{:S(2)}, u32[]{:S(2)}) collective-permute-start(f32[48,640]{1,0:T(8,128)S(1)} %get-tuple-element.22), channel_id=1, source_target_pairs={{0,3},{1,2},{2,1},{3,0},{4,7},{5,6},{6,5},{7,4},{8,11},{9,10},{10,... | collective-permute-start | bytes 368648 | tf_op jit(solution)/shard_map/ppermute | solution.py:207
  20.4 0.5 %collective-permute-start.6 = (f32[48,640]{1,0:T(8,128)S(1)}, f32[48,640]{1,0:T(8,128)S(1)}, u32[]{:S(2)}, u32[]{:S(2)}) collective-permute-start(f32[48,640]{1,0:T(8,128)S(1)} %get-tuple-element.22), channel_id=1, source_target_pairs={{0,2},{1,3},{2,0},{3,1},{4,5},{5,4},{6,7},{7,6},{8,10},{9,11},{10,... | collective-permute-start | bytes 368648 | tf_op jit(solution)/shard_map/ppermute | solution.py:207
  20.9 0.0 collective-permute-done.8.refs_0_
  20.9 0.0 collective-permute-start.9
  20.9 1.3 %collective-permute-done.9.refs_1_ = f32[8,3072]{1,0:T(8,128)S(1)} collective-permute-done((f32[8,3072]{1,0:T(8,128)S(1)}, f32[8,3072]{1,0:T(8,128)S(1)}, u32[]{:S(2)}, u32[]{:S(2)}) %collective-permute-start.9) | collective-permute-done | bytes 98336 | tf_op jit(solution)/shard_map/ppermute | solution.py:17
  22.2 1.2 %shard_map.52 = (f32[16,640]{1,0:T(8,128)S(1)}, bf16[32,3072]{1,0:T(8,128)(2,1)S(1)}) custom-call(f32[8,3072]{1,0:T(8,128)S(1)} %collective-permute-done.8.refs_0_, f32[8,3072]{1,0:T(8,128)S(1)} %collective-permute-done.9.refs_1_, bf16[3072,640]{1,0:T(8,128)(2,1)S(1)} %get-tuple-element.20.refs_6_.refs_2_, ...), custom_call_target="tpu_custom_call" | custom-call | flops 188743680 | bytes 1048576 | tf_op jit(solution)/shard_map/pallas_call | solution.py:92
  23.4 2.5 %collective-permute-start.12 = (f32[16,640]{1,0:T(8,128)S(1)}, f32[16,640]{1,0:T(8,128)S(1)}, u32[]{:S(2)}, u32[]{:S(2)}) collective-permute-start(f32[16,640]{1,0:T(8,128)S(1)} %get-tuple-element.26), channel_id=1, source_target_pairs={{0,3},{1,2},{2,1},{3,0},{4,7},{5,6},{6,5},{7,4},{8,11},{9,10},{10,... | collective-permute-start | bytes 122888 | tf_op jit(solution)/shard_map/ppermute | solution.py:207
  25.9 0.5 %collective-permute-start.11 = (f32[16,640]{1,0:T(8,128)S(1)}, f32[16,640]{1,0:T(8,128)S(1)}, u32[]{:S(2)}, u32[]{:S(2)}) collective-permute-start(f32[16,640]{1,0:T(8,128)S(1)} %get-tuple-element.26), channel_id=1, source_target_pairs={{0,2},{1,3},{2,0},{3,1},{4,5},{5,4},{6,7},{7,6},{8,10},{9,11},{10,... | collective-permute-start | bytes 122888 | tf_op jit(solution)/shard_map/ppermute | solution.py:207
  26.4 0.0 collective-permute-done.5
  26.4 0.5 %collective-permute-start.10 = (f32[16,640]{1,0:T(8,128)S(1)}, f32[16,640]{1,0:T(8,128)S(1)}, u32[]{:S(2)}, u32[]{:S(2)}) collective-permute-start(f32[16,640]{1,0:T(8,128)S(1)} %get-tuple-element.26), channel_id=1, source_target_pairs={{0,1},{1,0},{2,3},{3,2},{4,6},{5,7},{6,4},{7,5},{8,9},{9,8},{10,11... | collective-permute-start | bytes 122888 | tf_op jit(solution)/shard_map/ppermute | solution.py:207
  27.0 0.0 collective-permute-done.7
  27.0 0.2 collective-permute-done.6
  27.2 1.5 %shard_map.51 = (bf16[96,640]{1,0:T(8,128)(2,1)S(1)}, f32[8,3072]{1,0:T(8,128)S(1)}, f32[8,3072]{1,0:T(8,128)S(1)}, f32[8,3072]{1,0:T(8,128)S(1)}, f32[8,3072]{1...) custom-call(f32[48,640]{1,0:T(8,128)S(1)} %add.33.mine, f32[48,640]{1,0:T(8,128)S(1)} %add.34.theirs, ...), custom_call_target="tpu_custom_call" | custom-call | flops 566231040 | bytes 1048576 | tf_op jit(solution)/shard_map/pallas_call | solution.py:127
  28.7 0.1 collective-permute-start.13
  28.7 0.5 %collective-permute-start.15 = (f32[8,3072]{1,0:T(8,128)S(1)}, f32[8,3072]{1,0:T(8,128)S(1)}, u32[]{:S(2)}, u32[]{:S(2)}) collective-permute-start(f32[8,3072]{1,0:T(8,128)S(1)} %get-tuple-element.33), channel_id=1, source_target_pairs={{0,4},{4,0},{8,12},{12,8},{16,20},{20,16},{24,28},{28,24},{1,5},{5... | collective-permute-start | bytes 294920 | tf_op jit(solution)/shard_map/ppermute | solution.py:17
  29.2 1.2 %collective-permute-done.10 = f32[16,640]{1,0:T(8,128)S(1)} collective-permute-done((f32[16,640]{1,0:T(8,128)S(1)}, f32[16,640]{1,0:T(8,128)S(1)}, u32[]{:S(2)}, u32[]{:S(2)}) %collective-permute-start.10) | collective-permute-done | bytes 40992 | tf_op jit(solution)/shard_map/ppermute | solution.py:207
  30.5 0.0 collective-permute-done.12
  30.5 0.0 collective-permute-done.11
  30.5 1.2 %shard_map.53 = (bf16[32,640]{1,0:T(8,128)(2,1)S(1)}, f32[8,3072]{1,0:T(8,128)S(1)}, f32[8,3072]{1,0:T(8,128)S(1)}) custom-call(f32[16,640]{1,0:T(8,128)S(1)} %add.35.mine, f32[16,640]{1,0:T(8,128)S(1)} %add.36.theirs, f32[64,640]{1,0:T(8,128)S(1)} %copy-done, bf16[640,3072]{1,0:T(8,128)(2,1)S(1)} %get-tuple-element.23.hi, ...), custom_call_target="tpu_custom_call" | custom-call | flops 188743680 | bytes 1048576 | tf_op jit(solution)/shard_map/pallas_call | solution.py:127
  31.7 0.0 collective-permute-start.18
  31.7 0.5 %collective-permute-start.17 = (f32[8,3072]{1,0:T(8,128)S(1)}, f32[8,3072]{1,0:T(8,128)S(1)}, u32[]{:S(2)}, u32[]{:S(2)}) collective-permute-start(f32[8,3072]{1,0:T(8,128)S(1)} %get-tuple-element.35), channel_id=1, source_target_pairs={{0,4},{4,0},{8,12},{12,8},{16,20},{20,16},{24,28},{28,24},{1,5},{5... | collective-permute-start | bytes 294920 | tf_op jit(solution)/shard_map/ppermute | solution.py:17
  32.2 0.0 collective-permute-done.13
  32.2 2.7 %collective-permute-start.14 = (f32[8,3072]{1,0:T(8,128)S(1)}, f32[8,3072]{1,0:T(8,128)S(1)}, u32[]{:S(2)}, u32[]{:S(2)}) collective-permute-start(f32[8,3072]{1,0:T(8,128)S(1)} %add.37), channel_id=1, source_target_pairs={{0,16},{4,20},{8,24},{12,28},{16,0},{20,4},{24,8},{28,12},{1,17},{... | collective-permute-start | bytes 294920 | tf_op jit(solution)/shard_map/ppermute | solution.py:17
  35.0 0.0 collective-permute-done.15
  35.0 0.1 collective-permute-start.16
  35.1 0.0 collective-permute-done.18
  35.1 1.8 %collective-permute-start.19 = (f32[8,3072]{1,0:T(8,128)S(1)}, f32[8,3072]{1,0:T(8,128)S(1)}, u32[]{:S(2)}, u32[]{:S(2)}) collective-permute-start(f32[8,3072]{1,0:T(8,128)S(1)} %add.42), channel_id=1, source_target_pairs={{0,24},{4,28},{8,16},{12,20},{16,8},{20,12},{24,0},{28,4},{1,25},{... | collective-permute-start | bytes 294920 | tf_op jit(solution)/shard_map/ppermute | solution.py:17
  36.9 3.7 %gradient_jb.1 = f32[640,3072]{1,0:T(8,128)} custom-call(bf16[96,640]{1,0:T(8,128)(2,1)S(1)} %get-tuple-element.25.refs_0_, bf16[32,640]{1,0:T(8,128)(2,1)S(1)} %get-tuple-element.27.refs_1_, bf16[96,3072]{1,0:T(8,128)(2,1)S(1)} %get-tuple-element.28.refs_2_, bf16[32,3072]{1,0:T(8,128)(2,1)S(1)} %get-tuple-element.29.refs_3_), custom_call_target="tpu_custom_call" | custom-call | flops 754974720 | bytes 7864320 | tf_op jit(solution)/shard_map/gradient_jb/pallas_call | solution.py:168
  40.5 0.0 collective-permute-done.17
  40.5 0.7 %collective-permute-done.14 = f32[8,3072]{1,0:T(8,128)S(1)} collective-permute-done((f32[8,3072]{1,0:T(8,128)S(1)}, f32[8,3072]{1,0:T(8,128)S(1)}, u32[]{:S(2)}, u32[]{:S(2)}) %collective-permute-start.14) | collective-permute-done | bytes 98336 | tf_op jit(solution)/shard_map/ppermute | solution.py:17
  41.2 0.0 collective-permute-done.16
  41.2 2.1 %collective-permute-done.19 = f32[8,3072]{1,0:T(8,128)S(1)} collective-permute-done((f32[8,3072]{1,0:T(8,128)S(1)}, f32[8,3072]{1,0:T(8,128)S(1)}, u32[]{:S(2)}, u32[]{:S(2)}) %collective-permute-start.19) | collective-permute-done | bytes 98336 | tf_op jit(solution)/shard_map/ppermute | solution.py:17
  43.3 0.7 %add_add_fusion = f32[8,3072]{1,0:T(8,128)} fusion(f32[8,3072]{1,0:T(8,128)S(1)} %collective-permute-done.19, f32[8,3072]{1,0:T(8,128)S(1)} %get-tuple-element.34, f32[8,3072]{1,0:T(8,128)S(1)} %collective-permute-done.17, f32[8,3072]{1,0:T(8,128)S(1)} %collective-permute-done.14, f32[8,3072]{1,0:T(8,128)S(1)} %collective-permute-done.16), kind=kLoop, calls=%fused_computation | loop fusion | flops 98304 | bytes 589824 | tf_op jit(solution)/shard_map/add | solution.py:254
  (10 shorter events, 0.1 us)
Async XLA Ops:
  0.6 15.3 %copy-start.1 = (f32[8,3072]{1,0:T(8,128)S(1)}, f32[8,3072]{1,0:T(8,128)}, u32[]{:S(2)}) copy-start(f32[8,3072]{1,0:T(8,128)} %refs_4_.1) | copy-start | bytes 294916
  0.6 6.1 %collective-permute-start.2 = (f32[8,3072]{1,0:T(8,128)}, f32[8,3072]{1,0:T(8,128)S(1)}, u32[]{:S(2)}, u32[]{:S(2)}) collective-permute-start(f32[8,3072]{1,0:T(8,128)} %refs_4_.1), channel_id=1, source_target_pairs={{0,8},{4,12},{8,0},{12,4},{16,24},{20,28},{24,16},{28,20},{1,9},{5... | collective-permute-start | bytes 294920 | tf_op jit(solution)/shard_map/ppermute | solution.py:17
  3.8 7.5 %collective-permute-start = (f32[8,3072]{1,0:T(8,128)}, f32[8,3072]{1,0:T(8,128)S(1)}, u32[]{:S(2)}, u32[]{:S(2)}) collective-permute-start(f32[8,3072]{1,0:T(8,128)} %refs_4_.1), channel_id=1, source_target_pairs={{0,16},{4,20},{8,24},{12,28},{16,0},{20,4},{24,8},{28,12},{1,17},{... | collective-permute-start | bytes 294920 | tf_op jit(solution)/shard_map/ppermute | solution.py:17
  6.3 9.5 %collective-permute-start.4 = (f32[8,3072]{1,0:T(8,128)}, f32[8,3072]{1,0:T(8,128)S(1)}, u32[]{:S(2)}, u32[]{:S(2)}) collective-permute-start(f32[8,3072]{1,0:T(8,128)} %refs_4_.1), channel_id=1, source_target_pairs={{0,4},{4,0},{8,12},{12,8},{16,20},{20,16},{24,28},{28,24},{1,5},{5... | collective-permute-start | bytes 294920 | tf_op jit(solution)/shard_map/ppermute | solution.py:17
  6.8 9.1 %collective-permute-start.3 = (f32[8,3072]{1,0:T(8,128)S(1)}, f32[8,3072]{1,0:T(8,128)S(1)}, u32[]{:S(2)}, u32[]{:S(2)}) collective-permute-start(f32[8,3072]{1,0:T(8,128)S(1)} %collective-permute-done.2.refs_2_), channel_id=1, source_target_pairs={{0,4},{4,0},{8,12},{12,8},{16,20},{20,16},{24,28},{28,24},{1,5},{5... | collective-permute-start | bytes 294920 | tf_op jit(solution)/shard_map/ppermute | solution.py:17
  11.3 4.6 %collective-permute-start.1 = (f32[8,3072]{1,0:T(8,128)S(1)}, f32[8,3072]{1,0:T(8,128)S(1)}, u32[]{:S(2)}, u32[]{:S(2)}) collective-permute-start(f32[8,3072]{1,0:T(8,128)S(1)} %collective-permute-done.refs_0_), channel_id=1, source_target_pairs={{0,4},{4,0},{8,12},{12,8},{16,20},{20,16},{24,28},{28,24},{1,5},{5... | collective-permute-start | bytes 294920 | tf_op jit(solution)/shard_map/ppermute | solution.py:17
  11.3 9.7 %collective-permute-start.8 = (f32[8,3072]{1,0:T(8,128)S(1)}, f32[8,3072]{1,0:T(8,128)S(1)}, u32[]{:S(2)}, u32[]{:S(2)}) collective-permute-start(f32[8,3072]{1,0:T(8,128)S(1)} %collective-permute-done.refs_0_), channel_id=1, source_target_pairs={{0,8},{4,12},{8,0},{12,4},{16,24},{20,28},{24,16},{28,20},{1,9},{5... | collective-permute-start | bytes 294920 | tf_op jit(solution)/shard_map/ppermute | solution.py:17
  17.4 9.8 %copy-start = (f32[64,640]{1,0:T(8,128)S(1)}, f32[64,640]{1,0:T(8,128)}, u32[]{:S(2)}) copy-start(f32[64,640]{1,0:T(8,128)} %denom.3) | copy-start | bytes 491524
  17.4 9.1 %collective-permute-start.5 = (f32[48,640]{1,0:T(8,128)S(1)}, f32[48,640]{1,0:T(8,128)S(1)}, u32[]{:S(2)}, u32[]{:S(2)}) collective-permute-start(f32[48,640]{1,0:T(8,128)S(1)} %get-tuple-element.22), channel_id=1, source_target_pairs={{0,1},{1,0},{2,3},{3,2},{4,6},{5,7},{6,4},{7,5},{8,9},{9,8},{10,11... | collective-permute-start | bytes 368648 | tf_op jit(solution)/shard_map/ppermute | solution.py:207
  18.9 8.1 %collective-permute-start.7 = (f32[48,640]{1,0:T(8,128)S(1)}, f32[48,640]{1,0:T(8,128)S(1)}, u32[]{:S(2)}, u32[]{:S(2)}) collective-permute-start(f32[48,640]{1,0:T(8,128)S(1)} %get-tuple-element.22), channel_id=1, source_target_pairs={{0,3},{1,2},{2,1},{3,0},{4,7},{5,6},{6,5},{7,4},{8,11},{9,10},{10,... | collective-permute-start | bytes 368648 | tf_op jit(solution)/shard_map/ppermute | solution.py:207
  20.4 6.7 %collective-permute-start.6 = (f32[48,640]{1,0:T(8,128)S(1)}, f32[48,640]{1,0:T(8,128)S(1)}, u32[]{:S(2)}, u32[]{:S(2)}) collective-permute-start(f32[48,640]{1,0:T(8,128)S(1)} %get-tuple-element.22), channel_id=1, source_target_pairs={{0,2},{1,3},{2,0},{3,1},{4,5},{5,4},{6,7},{7,6},{8,10},{9,11},{10,... | collective-permute-start | bytes 368648 | tf_op jit(solution)/shard_map/ppermute | solution.py:207
  20.9 1.3 %collective-permute-start.9 = (f32[8,3072]{1,0:T(8,128)S(1)}, f32[8,3072]{1,0:T(8,128)S(1)}, u32[]{:S(2)}, u32[]{:S(2)}) collective-permute-start(f32[8,3072]{1,0:T(8,128)S(1)} %collective-permute-done.8.refs_0_), channel_id=1, source_target_pairs={{0,4},{4,0},{8,12},{12,8},{16,20},{20,16},{24,28},{28,24},{1,5},{5... | collective-permute-start | bytes 294920 | tf_op jit(solution)/shard_map/ppermute | solution.py:17
  23.4 7.0 %collective-permute-start.12 = (f32[16,640]{1,0:T(8,128)S(1)}, f32[16,640]{1,0:T(8,128)S(1)}, u32[]{:S(2)}, u32[]{:S(2)}) collective-permute-start(f32[16,640]{1,0:T(8,128)S(1)} %get-tuple-element.26), channel_id=1, source_target_pairs={{0,3},{1,2},{2,1},{3,0},{4,7},{5,6},{6,5},{7,4},{8,11},{9,10},{10,... | collective-permute-start | bytes 122888 | tf_op jit(solution)/shard_map/ppermute | solution.py:207
  25.9 4.5 %collective-permute-start.11 = (f32[16,640]{1,0:T(8,128)S(1)}, f32[16,640]{1,0:T(8,128)S(1)}, u32[]{:S(2)}, u32[]{:S(2)}) collective-permute-start(f32[16,640]{1,0:T(8,128)S(1)} %get-tuple-element.26), channel_id=1, source_target_pairs={{0,2},{1,3},{2,0},{3,1},{4,5},{5,4},{6,7},{7,6},{8,10},{9,11},{10,... | collective-permute-start | bytes 122888 | tf_op jit(solution)/shard_map/ppermute | solution.py:207
  26.4 4.0 %collective-permute-start.10 = (f32[16,640]{1,0:T(8,128)S(1)}, f32[16,640]{1,0:T(8,128)S(1)}, u32[]{:S(2)}, u32[]{:S(2)}) collective-permute-start(f32[16,640]{1,0:T(8,128)S(1)} %get-tuple-element.26), channel_id=1, source_target_pairs={{0,1},{1,0},{2,3},{3,2},{4,6},{5,7},{6,4},{7,5},{8,9},{9,8},{10,11... | collective-permute-start | bytes 122888 | tf_op jit(solution)/shard_map/ppermute | solution.py:207
  28.7 3.6 %collective-permute-start.13 = (f32[8,3072]{1,0:T(8,128)S(1)}, f32[8,3072]{1,0:T(8,128)S(1)}, u32[]{:S(2)}, u32[]{:S(2)}) collective-permute-start(f32[8,3072]{1,0:T(8,128)S(1)} %get-tuple-element.31), channel_id=1, source_target_pairs={{0,4},{4,0},{8,12},{12,8},{16,20},{20,16},{24,28},{28,24},{1,5},{5... | collective-permute-start | bytes 294920 | tf_op jit(solution)/shard_map/ppermute | solution.py:17
  28.7 6.2 %collective-permute-start.15 = (f32[8,3072]{1,0:T(8,128)S(1)}, f32[8,3072]{1,0:T(8,128)S(1)}, u32[]{:S(2)}, u32[]{:S(2)}) collective-permute-start(f32[8,3072]{1,0:T(8,128)S(1)} %get-tuple-element.33), channel_id=1, source_target_pairs={{0,4},{4,0},{8,12},{12,8},{16,20},{20,16},{24,28},{28,24},{1,5},{5... | collective-permute-start | bytes 294920 | tf_op jit(solution)/shard_map/ppermute | solution.py:17
  31.7 3.4 %collective-permute-start.18 = (f32[8,3072]{1,0:T(8,128)S(1)}, f32[8,3072]{1,0:T(8,128)S(1)}, u32[]{:S(2)}, u32[]{:S(2)}) collective-permute-start(f32[8,3072]{1,0:T(8,128)S(1)} %get-tuple-element.37), channel_id=1, source_target_pairs={{0,4},{4,0},{8,12},{12,8},{16,20},{20,16},{24,28},{28,24},{1,5},{5... | collective-permute-start | bytes 294920 | tf_op jit(solution)/shard_map/ppermute | solution.py:17
  31.7 8.8 %collective-permute-start.17 = (f32[8,3072]{1,0:T(8,128)S(1)}, f32[8,3072]{1,0:T(8,128)S(1)}, u32[]{:S(2)}, u32[]{:S(2)}) collective-permute-start(f32[8,3072]{1,0:T(8,128)S(1)} %get-tuple-element.35), channel_id=1, source_target_pairs={{0,4},{4,0},{8,12},{12,8},{16,20},{20,16},{24,28},{28,24},{1,5},{5... | collective-permute-start | bytes 294920 | tf_op jit(solution)/shard_map/ppermute | solution.py:17
  32.2 9.0 %collective-permute-start.14 = (f32[8,3072]{1,0:T(8,128)S(1)}, f32[8,3072]{1,0:T(8,128)S(1)}, u32[]{:S(2)}, u32[]{:S(2)}) collective-permute-start(f32[8,3072]{1,0:T(8,128)S(1)} %add.37), channel_id=1, source_target_pairs={{0,16},{4,20},{8,24},{12,28},{16,0},{20,4},{24,8},{28,12},{1,17},{... | collective-permute-start | bytes 294920 | tf_op jit(solution)/shard_map/ppermute | solution.py:17
  35.0 6.3 %collective-permute-start.16 = (f32[8,3072]{1,0:T(8,128)S(1)}, f32[8,3072]{1,0:T(8,128)S(1)}, u32[]{:S(2)}, u32[]{:S(2)}) collective-permute-start(f32[8,3072]{1,0:T(8,128)S(1)} %add.38), channel_id=1, source_target_pairs={{0,8},{4,12},{8,0},{12,4},{16,24},{20,28},{24,16},{28,20},{1,9},{5... | collective-permute-start | bytes 294920 | tf_op jit(solution)/shard_map/ppermute | solution.py:17
  35.1 8.2 %collective-permute-start.19 = (f32[8,3072]{1,0:T(8,128)S(1)}, f32[8,3072]{1,0:T(8,128)S(1)}, u32[]{:S(2)}, u32[]{:S(2)}) collective-permute-start(f32[8,3072]{1,0:T(8,128)S(1)} %add.42), channel_id=1, source_target_pairs={{0,24},{4,28},{8,16},{12,20},{16,8},{20,12},{24,0},{28,4},{1,25},{... | collective-permute-start | bytes 294920 | tf_op jit(solution)/shard_map/ppermute | solution.py:17

commit v6 on v5

--- a/solution.py
+++ b/solution.py
@@ -35,7 +35,7 @@
     height, width = factor_jb.shape
     piece = width_of(height, 128)
     pieces = height // piece
-    step = width_of(width, 1024)
+    step = width_of(width, 256)
 
     def kernel(jb, hi, lo, hi_t, lo_t, held, sems):
         def copy(p):
@@ -73,7 +73,7 @@
     height, width = blocks[0].shape
     rows = n * height
     columns = hi_t.shape[1]
-    tile = width_of(columns, 128)
+    tile = width_of(columns, 640)
 
     def kernel(*refs):
         block_refs, (hi, lo, out, parts) = refs[:n], refs[n:]
@@ -199,7 +199,7 @@
 
     def partner(row, column):
         if straight(aux):
-            return row * aux + (column ^ ((1, 2, 3), (2, 1, 3))[row % 2][step])
+            return row * aux + (column ^ ((3, 1, 2), (3, 2, 1))[row % 2][step])
         bit = (step + row % 2 * (steps // 2)) % steps
         return row * aux + (column ^ 1 << bit)
 

time: 44.1 us -> 45 us (1.020)
  waiting for transfers between devices: 10.3 us -> 11.2 us
    ppermute x6, waiting for transfers between devices: 1.37 us -> 2.3 us  [exchange(): return lax.ppermute(x, ('row', 'aux'), pairs)]
  transfers between devices with their start and end apart: 20 -> 20, of which waited for: 7 -> 6; matrix products, arithmetic and copies ran while one was open for 0% -> 0% of each run, Pallas kernels for 30% -> 29%
where the time goes in v6:
time: 45 us; the launch traced here: 44.9 us
  starting transfers between devices  18.9 us (42%)
  Pallas kernels  13.2 us (29%)
  waiting for transfers between devices  11.2 us (25%)
  between operations  0.81 us (2%)
  other arithmetic  0.76 us (2%)
    ppermute x14, starting transfers between devices, swap(): return lax.ppermute(x, axis, [(i, i ^ distance) for i in range(size)])  11.8 us
    ppermute x14, waiting for transfers between devices, swap(): return lax.ppermute(x, axis, [(i, i ^ distance) for i in range(size)])  8.93 us
    ppermute x6, starting transfers between devices, exchange(): return lax.ppermute(x, ('row', 'aux'), pairs)  7.1 us
    pallas_call x1, Pallas kernels, prepare(): pl.pallas_call(kernel, name='prepare', out_shape=(plain, plain, turned, t...  4.18 us
    pallas_call x1, Pallas kernels, gradient_jb(): pl.pallas_call(kernel, name='gradient_jb', out_shape=jax.ShapeDtypeStruct...  3.66 us
    pallas_call x2, Pallas kernels, gradient_share(): pl.pallas_call(kernel, out_shape=(jax.ShapeDtypeStruct((2 * rows, columns...  2.67 us
    pallas_call x2, Pallas kernels, integral_share(): pl.pallas_call(kernel, out_shape=(jax.ShapeDtypeStruct((rows, columns), F...  2.64 us
    ppermute x6, waiting for transfers between devices, exchange(): return lax.ppermute(x, ('row', 'aux'), pairs)  2.3 us
  transfers between devices with their start and end apart: 20, of which 6 were waited for; matrix products, arithmetic and copies ran while one was open for 0% of the time, Pallas kernels for 29%

profile of v6, /device:TPU:0, one launch (start us, length us, event | category | flops | bytes accessed | tf_op | source)
XLA Modules:
  0.0 44.9 jit_solution(9396834203015850895)
XLA Ops:
  0.6 3.1 %collective-permute-start.2 = (f32[8,3072]{1,0:T(8,128)}, f32[8,3072]{1,0:T(8,128)S(1)}, u32[]{:S(2)}, u32[]{:S(2)}) collective-permute-start(f32[8,3072]{1,0:T(8,128)} %refs_4_.1), channel_id=1, source_target_pairs={{0,8},{4,12},{8,0},{12,4},{16,24},{20,28},{24,16},{28,20},{1,9},{5... | collective-permute-start | bytes 294920 | tf_op jit(solution)/shard_map/ppermute | solution.py:17
  3.8 2.6 %collective-permute-start = (f32[8,3072]{1,0:T(8,128)}, f32[8,3072]{1,0:T(8,128)S(1)}, u32[]{:S(2)}, u32[]{:S(2)}) collective-permute-start(f32[8,3072]{1,0:T(8,128)} %refs_4_.1), channel_id=1, source_target_pairs={{0,16},{4,20},{8,24},{12,28},{16,0},{20,4},{24,8},{28,12},{1,17},{... | collective-permute-start | bytes 294920 | tf_op jit(solution)/shard_map/ppermute | solution.py:17
  6.3 0.0 collective-permute-start.4
  6.3 0.4 collective-permute-done.2.refs_2_
  6.8 0.1 collective-permute-start.3
  6.9 4.4 %collective-permute-done.refs_0_ = f32[8,3072]{1,0:T(8,128)S(1)} collective-permute-done((f32[8,3072]{1,0:T(8,128)}, f32[8,3072]{1,0:T(8,128)S(1)}, u32[]{:S(2)}, u32[]{:S(2)}) %collective-permute-start) | collective-permute-done | bytes 98336 | tf_op jit(solution)/shard_map/ppermute | solution.py:17
  11.3 0.0 collective-permute-start.1
  11.3 0.3 collective-permute-start.8
  11.6 4.2 %prepare.1 = (bf16[640,3072]{1,0:T(8,128)(2,1)S(1)}, bf16[640,3072]{1,0:T(8,128)(2,1)S(1)}, bf16[3072,640]{1,0:T(8,128)(2,1)S(1)}, bf16[3072,640]{1,0:T(8,128)(2,1)S(1)}) custom-call(f32[640,3072]{1,0:T(8,128)} %jb.1), custom_call_target="tpu_custom_call" | custom-call | flops 7864320 | bytes 7864320 | tf_op jit(solution)/shard_map/prepare/pallas_call | solution.py:59
  15.8 0.0 collective-permute-done.4.refs_5_
  15.8 0.0 collective-permute-done.3.refs_3_
  15.8 0.0 collective-permute-done.1.refs_1_
  15.9 1.4 %shard_map.50 = (f32[48,640]{1,0:T(8,128)S(1)}, bf16[96,3072]{1,0:T(8,128)(2,1)S(1)}) custom-call(f32[8,3072]{1,0:T(8,128)S(1)} %collective-permute-done.refs_0_, f32[8,3072]{1,0:T(8,128)S(1)} %collective-permute-done.1.refs_1_, f32[8,3072]{1,0:T(8,128)S(1)} %collective-permute-done.2.refs_2_, f32[8,3072]{1,0:T(8,128)S(1)} %collective-permute-done.3.refs_3_, ...), custom_call_target="tpu_custom_call" | custom-call | flops 566231040 | bytes 1048576 | tf_op jit(solution)/shard_map/pallas_call | solution.py:92
  17.3 0.0 copy-start
  17.3 2.5 %collective-permute-start.5 = (f32[48,640]{1,0:T(8,128)S(1)}, f32[48,640]{1,0:T(8,128)S(1)}, u32[]{:S(2)}, u32[]{:S(2)}) collective-permute-start(f32[48,640]{1,0:T(8,128)S(1)} %get-tuple-element.22), channel_id=1, source_target_pairs={{0,3},{1,2},{2,1},{3,0},{4,7},{5,6},{6,5},{7,4},{8,11},{9,10},{10,... | collective-permute-start | bytes 368648 | tf_op jit(solution)/shard_map/ppermute | solution.py:207
  19.8 0.5 %collective-permute-start.7 = (f32[48,640]{1,0:T(8,128)S(1)}, f32[48,640]{1,0:T(8,128)S(1)}, u32[]{:S(2)}, u32[]{:S(2)}) collective-permute-start(f32[48,640]{1,0:T(8,128)S(1)} %get-tuple-element.22), channel_id=1, source_target_pairs={{0,2},{1,3},{2,0},{3,1},{4,5},{5,4},{6,7},{7,6},{8,10},{9,11},{10,... | collective-permute-start | bytes 368648 | tf_op jit(solution)/shard_map/ppermute | solution.py:207
  20.3 0.6 %collective-permute-start.6 = (f32[48,640]{1,0:T(8,128)S(1)}, f32[48,640]{1,0:T(8,128)S(1)}, u32[]{:S(2)}, u32[]{:S(2)}) collective-permute-start(f32[48,640]{1,0:T(8,128)S(1)} %get-tuple-element.22), channel_id=1, source_target_pairs={{0,1},{1,0},{2,3},{3,2},{4,6},{5,7},{6,4},{7,5},{8,9},{9,8},{10,11... | collective-permute-start | bytes 368648 | tf_op jit(solution)/shard_map/ppermute | solution.py:207
  20.9 0.0 collective-permute-done.8.refs_0_
  20.9 0.0 collective-permute-start.9
  20.9 1.3 %collective-permute-done.9.refs_1_ = f32[8,3072]{1,0:T(8,128)S(1)} collective-permute-done((f32[8,3072]{1,0:T(8,128)S(1)}, f32[8,3072]{1,0:T(8,128)S(1)}, u32[]{:S(2)}, u32[]{:S(2)}) %collective-permute-start.9) | collective-permute-done | bytes 98336 | tf_op jit(solution)/shard_map/ppermute | solution.py:17
  22.2 1.2 %shard_map.52 = (f32[16,640]{1,0:T(8,128)S(1)}, bf16[32,3072]{1,0:T(8,128)(2,1)S(1)}) custom-call(f32[8,3072]{1,0:T(8,128)S(1)} %collective-permute-done.8.refs_0_, f32[8,3072]{1,0:T(8,128)S(1)} %collective-permute-done.9.refs_1_, bf16[3072,640]{1,0:T(8,128)(2,1)S(1)} %get-tuple-element.20.refs_6_.refs_2_, ...), custom_call_target="tpu_custom_call" | custom-call | flops 188743680 | bytes 1048576 | tf_op jit(solution)/shard_map/pallas_call | solution.py:92
  23.4 1.6 %collective-permute-start.12 = (f32[16,640]{1,0:T(8,128)S(1)}, f32[16,640]{1,0:T(8,128)S(1)}, u32[]{:S(2)}, u32[]{:S(2)}) collective-permute-start(f32[16,640]{1,0:T(8,128)S(1)} %get-tuple-element.26), channel_id=1, source_target_pairs={{0,2},{1,3},{2,0},{3,1},{4,5},{5,4},{6,7},{7,6},{8,10},{9,11},{10,... | collective-permute-start | bytes 122888 | tf_op jit(solution)/shard_map/ppermute | solution.py:207
  24.9 1.5 %collective-permute-start.11 = (f32[16,640]{1,0:T(8,128)S(1)}, f32[16,640]{1,0:T(8,128)S(1)}, u32[]{:S(2)}, u32[]{:S(2)}) collective-permute-start(f32[16,640]{1,0:T(8,128)S(1)} %get-tuple-element.26), channel_id=1, source_target_pairs={{0,1},{1,0},{2,3},{3,2},{4,6},{5,7},{6,4},{7,5},{8,9},{9,8},{10,11... | collective-permute-start | bytes 122888 | tf_op jit(solution)/shard_map/ppermute | solution.py:207
  26.4 0.0 collective-permute-done.5
  26.4 0.5 %collective-permute-start.10 = (f32[16,640]{1,0:T(8,128)S(1)}, f32[16,640]{1,0:T(8,128)S(1)}, u32[]{:S(2)}, u32[]{:S(2)}) collective-permute-start(f32[16,640]{1,0:T(8,128)S(1)} %get-tuple-element.26), channel_id=1, source_target_pairs={{0,3},{1,2},{2,1},{3,0},{4,7},{5,6},{6,5},{7,4},{8,11},{9,10},{10,... | collective-permute-start | bytes 122888 | tf_op jit(solution)/shard_map/ppermute | solution.py:207
  26.9 0.0 collective-permute-done.7
  27.0 0.0 collective-permute-done.6
  27.0 1.5 %shard_map.51 = (bf16[96,640]{1,0:T(8,128)(2,1)S(1)}, f32[8,3072]{1,0:T(8,128)S(1)}, f32[8,3072]{1,0:T(8,128)S(1)}, f32[8,3072]{1,0:T(8,128)S(1)}, f32[8,3072]{1...) custom-call(f32[48,640]{1,0:T(8,128)S(1)} %add.33.mine, f32[48,640]{1,0:T(8,128)S(1)} %add.34.theirs, ...), custom_call_target="tpu_custom_call" | custom-call | flops 566231040 | bytes 1048576 | tf_op jit(solution)/shard_map/pallas_call | solution.py:127
  28.5 0.1 collective-permute-start.13
  28.5 0.5 %collective-permute-start.15 = (f32[8,3072]{1,0:T(8,128)S(1)}, f32[8,3072]{1,0:T(8,128)S(1)}, u32[]{:S(2)}, u32[]{:S(2)}) collective-permute-start(f32[8,3072]{1,0:T(8,128)S(1)} %get-tuple-element.33), channel_id=1, source_target_pairs={{0,4},{4,0},{8,12},{12,8},{16,20},{20,16},{24,28},{28,24},{1,5},{5... | collective-permute-start | bytes 294920 | tf_op jit(solution)/shard_map/ppermute | solution.py:17
  29.0 2.3 %collective-permute-done.10 = f32[16,640]{1,0:T(8,128)S(1)} collective-permute-done((f32[16,640]{1,0:T(8,128)S(1)}, f32[16,640]{1,0:T(8,128)S(1)}, u32[]{:S(2)}, u32[]{:S(2)}) %collective-permute-start.10) | collective-permute-done | bytes 40992 | tf_op jit(solution)/shard_map/ppermute | solution.py:207
  31.3 0.0 collective-permute-done.12
  31.3 0.0 collective-permute-done.11
  31.4 1.2 %shard_map.53 = (bf16[32,640]{1,0:T(8,128)(2,1)S(1)}, f32[8,3072]{1,0:T(8,128)S(1)}, f32[8,3072]{1,0:T(8,128)S(1)}) custom-call(f32[16,640]{1,0:T(8,128)S(1)} %add.35.mine, f32[16,640]{1,0:T(8,128)S(1)} %add.36.theirs, f32[64,640]{1,0:T(8,128)S(1)} %copy-done, bf16[640,3072]{1,0:T(8,128)(2,1)S(1)} %get-tuple-element.23.hi, ...), custom_call_target="tpu_custom_call" | custom-call | flops 188743680 | bytes 1048576 | tf_op jit(solution)/shard_map/pallas_call | solution.py:127
  32.6 0.0 collective-permute-start.18
  32.6 0.5 %collective-permute-start.17 = (f32[8,3072]{1,0:T(8,128)S(1)}, f32[8,3072]{1,0:T(8,128)S(1)}, u32[]{:S(2)}, u32[]{:S(2)}) collective-permute-start(f32[8,3072]{1,0:T(8,128)S(1)} %get-tuple-element.35), channel_id=1, source_target_pairs={{0,4},{4,0},{8,12},{12,8},{16,20},{20,16},{24,28},{28,24},{1,5},{5... | collective-permute-start | bytes 294920 | tf_op jit(solution)/shard_map/ppermute | solution.py:17
  33.1 0.0 collective-permute-done.13
  33.1 2.7 %collective-permute-start.14 = (f32[8,3072]{1,0:T(8,128)S(1)}, f32[8,3072]{1,0:T(8,128)S(1)}, u32[]{:S(2)}, u32[]{:S(2)}) collective-permute-start(f32[8,3072]{1,0:T(8,128)S(1)} %add.37), channel_id=1, source_target_pairs={{0,16},{4,20},{8,24},{12,28},{16,0},{20,4},{24,8},{28,12},{1,17},{... | collective-permute-start | bytes 294920 | tf_op jit(solution)/shard_map/ppermute | solution.py:17
  35.8 0.0 collective-permute-done.15
  35.9 0.1 collective-permute-start.16
  36.0 0.0 collective-permute-done.18
  36.0 1.8 %collective-permute-start.19 = (f32[8,3072]{1,0:T(8,128)S(1)}, f32[8,3072]{1,0:T(8,128)S(1)}, u32[]{:S(2)}, u32[]{:S(2)}) collective-permute-start(f32[8,3072]{1,0:T(8,128)S(1)} %add.42), channel_id=1, source_target_pairs={{0,24},{4,28},{8,16},{12,20},{16,8},{20,12},{24,0},{28,4},{1,25},{... | collective-permute-start | bytes 294920 | tf_op jit(solution)/shard_map/ppermute | solution.py:17
  37.7 3.7 %gradient_jb.1 = f32[640,3072]{1,0:T(8,128)} custom-call(bf16[96,640]{1,0:T(8,128)(2,1)S(1)} %get-tuple-element.25.refs_0_, bf16[32,640]{1,0:T(8,128)(2,1)S(1)} %get-tuple-element.27.refs_1_, bf16[96,3072]{1,0:T(8,128)(2,1)S(1)} %get-tuple-element.28.refs_2_, bf16[32,3072]{1,0:T(8,128)(2,1)S(1)} %get-tuple-element.29.refs_3_), custom_call_target="tpu_custom_call" | custom-call | flops 754974720 | bytes 7864320 | tf_op jit(solution)/shard_map/gradient_jb/pallas_call | solution.py:168
  41.4 0.0 collective-permute-done.17
  41.4 0.7 %collective-permute-done.14 = f32[8,3072]{1,0:T(8,128)S(1)} collective-permute-done((f32[8,3072]{1,0:T(8,128)S(1)}, f32[8,3072]{1,0:T(8,128)S(1)}, u32[]{:S(2)}, u32[]{:S(2)}) %collective-permute-start.14) | collective-permute-done | bytes 98336 | tf_op jit(solution)/shard_map/ppermute | solution.py:17
  42.1 0.0 collective-permute-done.16
  42.1 2.1 %collective-permute-done.19 = f32[8,3072]{1,0:T(8,128)S(1)} collective-permute-done((f32[8,3072]{1,0:T(8,128)S(1)}, f32[8,3072]{1,0:T(8,128)S(1)}, u32[]{:S(2)}, u32[]{:S(2)}) %collective-permute-start.19) | collective-permute-done | bytes 98336 | tf_op jit(solution)/shard_map/ppermute | solution.py:17
  44.2 0.7 %add_add_fusion = f32[8,3072]{1,0:T(8,128)} fusion(f32[8,3072]{1,0:T(8,128)S(1)} %collective-permute-done.19, f32[8,3072]{1,0:T(8,128)S(1)} %get-tuple-element.34, f32[8,3072]{1,0:T(8,128)S(1)} %collective-permute-done.17, f32[8,3072]{1,0:T(8,128)S(1)} %collective-permute-done.14, f32[8,3072]{1,0:T(8,128)S(1)} %collective-permute-done.16), kind=kLoop, calls=%fused_computation | loop fusion | flops 98304 | bytes 589824 | tf_op jit(solution)/shard_map/add | solution.py:254
  (10 shorter events, 0.1 us)
Async XLA Ops:
  0.6 15.2 %copy-start.1 = (f32[8,3072]{1,0:T(8,128)S(1)}, f32[8,3072]{1,0:T(8,128)}, u32[]{:S(2)}) copy-start(f32[8,3072]{1,0:T(8,128)} %refs_4_.1) | copy-start | bytes 294916
  0.6 6.1 %collective-permute-start.2 = (f32[8,3072]{1,0:T(8,128)}, f32[8,3072]{1,0:T(8,128)S(1)}, u32[]{:S(2)}, u32[]{:S(2)}) collective-permute-start(f32[8,3072]{1,0:T(8,128)} %refs_4_.1), channel_id=1, source_target_pairs={{0,8},{4,12},{8,0},{12,4},{16,24},{20,28},{24,16},{28,20},{1,9},{5... | collective-permute-start | bytes 294920 | tf_op jit(solution)/shard_map/ppermute | solution.py:17
  3.8 7.5 %collective-permute-start = (f32[8,3072]{1,0:T(8,128)}, f32[8,3072]{1,0:T(8,128)S(1)}, u32[]{:S(2)}, u32[]{:S(2)}) collective-permute-start(f32[8,3072]{1,0:T(8,128)} %refs_4_.1), channel_id=1, source_target_pairs={{0,16},{4,20},{8,24},{12,28},{16,0},{20,4},{24,8},{28,12},{1,17},{... | collective-permute-start | bytes 294920 | tf_op jit(solution)/shard_map/ppermute | solution.py:17
  6.3 9.5 %collective-permute-start.4 = (f32[8,3072]{1,0:T(8,128)}, f32[8,3072]{1,0:T(8,128)S(1)}, u32[]{:S(2)}, u32[]{:S(2)}) collective-permute-start(f32[8,3072]{1,0:T(8,128)} %refs_4_.1), channel_id=1, source_target_pairs={{0,4},{4,0},{8,12},{12,8},{16,20},{20,16},{24,28},{28,24},{1,5},{5... | collective-permute-start | bytes 294920 | tf_op jit(solution)/shard_map/ppermute | solution.py:17
  6.8 9.1 %collective-permute-start.3 = (f32[8,3072]{1,0:T(8,128)S(1)}, f32[8,3072]{1,0:T(8,128)S(1)}, u32[]{:S(2)}, u32[]{:S(2)}) collective-permute-start(f32[8,3072]{1,0:T(8,128)S(1)} %collective-permute-done.2.refs_2_), channel_id=1, source_target_pairs={{0,4},{4,0},{8,12},{12,8},{16,20},{20,16},{24,28},{28,24},{1,5},{5... | collective-permute-start | bytes 294920 | tf_op jit(solution)/shard_map/ppermute | solution.py:17
  11.3 4.5 %collective-permute-start.1 = (f32[8,3072]{1,0:T(8,128)S(1)}, f32[8,3072]{1,0:T(8,128)S(1)}, u32[]{:S(2)}, u32[]{:S(2)}) collective-permute-start(f32[8,3072]{1,0:T(8,128)S(1)} %collective-permute-done.refs_0_), channel_id=1, source_target_pairs={{0,4},{4,0},{8,12},{12,8},{16,20},{20,16},{24,28},{28,24},{1,5},{5... | collective-permute-start | bytes 294920 | tf_op jit(solution)/shard_map/ppermute | solution.py:17
  11.3 9.6 %collective-permute-start.8 = (f32[8,3072]{1,0:T(8,128)S(1)}, f32[8,3072]{1,0:T(8,128)S(1)}, u32[]{:S(2)}, u32[]{:S(2)}) collective-permute-start(f32[8,3072]{1,0:T(8,128)S(1)} %collective-permute-done.refs_0_), channel_id=1, source_target_pairs={{0,8},{4,12},{8,0},{12,4},{16,24},{20,28},{24,16},{28,20},{1,9},{5... | collective-permute-start | bytes 294920 | tf_op jit(solution)/shard_map/ppermute | solution.py:17
  17.3 9.7 %copy-start = (f32[64,640]{1,0:T(8,128)S(1)}, f32[64,640]{1,0:T(8,128)}, u32[]{:S(2)}) copy-start(f32[64,640]{1,0:T(8,128)} %denom.3) | copy-start | bytes 491524
  17.3 9.1 %collective-permute-start.5 = (f32[48,640]{1,0:T(8,128)S(1)}, f32[48,640]{1,0:T(8,128)S(1)}, u32[]{:S(2)}, u32[]{:S(2)}) collective-permute-start(f32[48,640]{1,0:T(8,128)S(1)} %get-tuple-element.22), channel_id=1, source_target_pairs={{0,3},{1,2},{2,1},{3,0},{4,7},{5,6},{6,5},{7,4},{8,11},{9,10},{10,... | collective-permute-start | bytes 368648 | tf_op jit(solution)/shard_map/ppermute | solution.py:207
  19.8 7.2 %collective-permute-start.7 = (f32[48,640]{1,0:T(8,128)S(1)}, f32[48,640]{1,0:T(8,128)S(1)}, u32[]{:S(2)}, u32[]{:S(2)}) collective-permute-start(f32[48,640]{1,0:T(8,128)S(1)} %get-tuple-element.22), channel_id=1, source_target_pairs={{0,2},{1,3},{2,0},{3,1},{4,5},{5,4},{6,7},{7,6},{8,10},{9,11},{10,... | collective-permute-start | bytes 368648 | tf_op jit(solution)/shard_map/ppermute | solution.py:207
  20.3 6.7 %collective-permute-start.6 = (f32[48,640]{1,0:T(8,128)S(1)}, f32[48,640]{1,0:T(8,128)S(1)}, u32[]{:S(2)}, u32[]{:S(2)}) collective-permute-start(f32[48,640]{1,0:T(8,128)S(1)} %get-tuple-element.22), channel_id=1, source_target_pairs={{0,1},{1,0},{2,3},{3,2},{4,6},{5,7},{6,4},{7,5},{8,9},{9,8},{10,11... | collective-permute-start | bytes 368648 | tf_op jit(solution)/shard_map/ppermute | solution.py:207
  20.9 1.3 %collective-permute-start.9 = (f32[8,3072]{1,0:T(8,128)S(1)}, f32[8,3072]{1,0:T(8,128)S(1)}, u32[]{:S(2)}, u32[]{:S(2)}) collective-permute-start(f32[8,3072]{1,0:T(8,128)S(1)} %collective-permute-done.8.refs_0_), channel_id=1, source_target_pairs={{0,4},{4,0},{8,12},{12,8},{16,20},{20,16},{24,28},{28,24},{1,5},{5... | collective-permute-start | bytes 294920 | tf_op jit(solution)/shard_map/ppermute | solution.py:17
  23.4 8.0 %collective-permute-start.12 = (f32[16,640]{1,0:T(8,128)S(1)}, f32[16,640]{1,0:T(8,128)S(1)}, u32[]{:S(2)}, u32[]{:S(2)}) collective-permute-start(f32[16,640]{1,0:T(8,128)S(1)} %get-tuple-element.26), channel_id=1, source_target_pairs={{0,2},{1,3},{2,0},{3,1},{4,5},{5,4},{6,7},{7,6},{8,10},{9,11},{10,... | collective-permute-start | bytes 122888 | tf_op jit(solution)/shard_map/ppermute | solution.py:207
  24.9 6.4 %collective-permute-start.11 = (f32[16,640]{1,0:T(8,128)S(1)}, f32[16,640]{1,0:T(8,128)S(1)}, u32[]{:S(2)}, u32[]{:S(2)}) collective-permute-start(f32[16,640]{1,0:T(8,128)S(1)} %get-tuple-element.26), channel_id=1, source_target_pairs={{0,1},{1,0},{2,3},{3,2},{4,6},{5,7},{6,4},{7,5},{8,9},{9,8},{10,11... | collective-permute-start | bytes 122888 | tf_op jit(solution)/shard_map/ppermute | solution.py:207
  26.4 4.9 %collective-permute-start.10 = (f32[16,640]{1,0:T(8,128)S(1)}, f32[16,640]{1,0:T(8,128)S(1)}, u32[]{:S(2)}, u32[]{:S(2)}) collective-permute-start(f32[16,640]{1,0:T(8,128)S(1)} %get-tuple-element.26), channel_id=1, source_target_pairs={{0,3},{1,2},{2,1},{3,0},{4,7},{5,6},{6,5},{7,4},{8,11},{9,10},{10,... | collective-permute-start | bytes 122888 | tf_op jit(solution)/shard_map/ppermute | solution.py:207
  28.5 4.6 %collective-permute-start.13 = (f32[8,3072]{1,0:T(8,128)S(1)}, f32[8,3072]{1,0:T(8,128)S(1)}, u32[]{:S(2)}, u32[]{:S(2)}) collective-permute-start(f32[8,3072]{1,0:T(8,128)S(1)} %get-tuple-element.31), channel_id=1, source_target_pairs={{0,4},{4,0},{8,12},{12,8},{16,20},{20,16},{24,28},{28,24},{1,5},{5... | collective-permute-start | bytes 294920 | tf_op jit(solution)/shard_map/ppermute | solution.py:17
  28.5 7.3 %collective-permute-start.15 = (f32[8,3072]{1,0:T(8,128)S(1)}, f32[8,3072]{1,0:T(8,128)S(1)}, u32[]{:S(2)}, u32[]{:S(2)}) collective-permute-start(f32[8,3072]{1,0:T(8,128)S(1)} %get-tuple-element.33), channel_id=1, source_target_pairs={{0,4},{4,0},{8,12},{12,8},{16,20},{20,16},{24,28},{28,24},{1,5},{5... | collective-permute-start | bytes 294920 | tf_op jit(solution)/shard_map/ppermute | solution.py:17
  32.6 3.4 %collective-permute-start.18 = (f32[8,3072]{1,0:T(8,128)S(1)}, f32[8,3072]{1,0:T(8,128)S(1)}, u32[]{:S(2)}, u32[]{:S(2)}) collective-permute-start(f32[8,3072]{1,0:T(8,128)S(1)} %get-tuple-element.37), channel_id=1, source_target_pairs={{0,4},{4,0},{8,12},{12,8},{16,20},{20,16},{24,28},{28,24},{1,5},{5... | collective-permute-start | bytes 294920 | tf_op jit(solution)/shard_map/ppermute | solution.py:17
  32.6 8.8 %collective-permute-start.17 = (f32[8,3072]{1,0:T(8,128)S(1)}, f32[8,3072]{1,0:T(8,128)S(1)}, u32[]{:S(2)}, u32[]{:S(2)}) collective-permute-start(f32[8,3072]{1,0:T(8,128)S(1)} %get-tuple-element.35), channel_id=1, source_target_pairs={{0,4},{4,0},{8,12},{12,8},{16,20},{20,16},{24,28},{28,24},{1,5},{5... | collective-permute-start | bytes 294920 | tf_op jit(solution)/shard_map/ppermute | solution.py:17
  33.1 9.0 %collective-permute-start.14 = (f32[8,3072]{1,0:T(8,128)S(1)}, f32[8,3072]{1,0:T(8,128)S(1)}, u32[]{:S(2)}, u32[]{:S(2)}) collective-permute-start(f32[8,3072]{1,0:T(8,128)S(1)} %add.37), channel_id=1, source_target_pairs={{0,16},{4,20},{8,24},{12,28},{16,0},{20,4},{24,8},{28,12},{1,17},{... | collective-permute-start | bytes 294920 | tf_op jit(solution)/shard_map/ppermute | solution.py:17
  35.9 6.3 %collective-permute-start.16 = (f32[8,3072]{1,0:T(8,128)S(1)}, f32[8,3072]{1,0:T(8,128)S(1)}, u32[]{:S(2)}, u32[]{:S(2)}) collective-permute-start(f32[8,3072]{1,0:T(8,128)S(1)} %add.38), channel_id=1, source_target_pairs={{0,8},{4,12},{8,0},{12,4},{16,24},{20,28},{24,16},{28,20},{1,9},{5... | collective-permute-start | bytes 294920 | tf_op jit(solution)/shard_map/ppermute | solution.py:17
  36.0 8.2 %collective-permute-start.19 = (f32[8,3072]{1,0:T(8,128)S(1)}, f32[8,3072]{1,0:T(8,128)S(1)}, u32[]{:S(2)}, u32[]{:S(2)}) collective-permute-start(f32[8,3072]{1,0:T(8,128)S(1)} %add.42), channel_id=1, source_target_pairs={{0,24},{4,28},{8,16},{12,20},{16,8},{20,12},{24,0},{28,4},{1,25},{... | collective-permute-start | bytes 294920 | tf_op jit(solution)/shard_map/ppermute | solution.py:17
